TPU v7x, 128 devices: a whole 4x4x4 slice. The times are simulated.
128 devices in a mesh: dom: 128 (over y, z, x, core).
Axes of the slice: x: 4, y: 4, z: 4, core: 2. Of those that a mesh axis runs over, the one named last changes fastest.
Arguments:
- element_freedom_values: float32 [9, 20, 131072], P(None, None, 'dom'), may hold values from -6 to 6
- scaled_jacobian_matrices: float32 [3, 9, 9, 131072], P(None, None, None, 'dom'), may hold values from -2 to 2
- outward_face_normals: float32 [4, 3, 131072], P(None, None, 'dom'), may hold values from -3 to 3
- largest_wave_speed: float32 [131072], P('dom'), may hold values from 0.5 to 2
- element_cluster_index: int32 [131072], P('dom'), may hold values 0 or 1
- element_new_slot: int32 [131072], P('dom'), may hold values from 0 to 147455, as said below
- neighbours: int32 [4, 131072], P(None, 'dom'), may hold values from 0 to 147199, as said below
- face_rotation_codes: int32 [4, 131072], P(None, 'dom'), may hold values from 0 to 11
- deriv_mats: float32 [3, 20, 20], replicated, may hold values from -1.25 to 1.25
- stiff_mats: float32 [3, 20, 20], replicated, may hold values from -1.25 to 1.25
- face_eval: float32 [12, 20, 16], replicated, may hold values from -1.25 to 1.25
- face_lift: float32 [4, 16, 20], replicated, may hold values from -1.5 to 1.5
Outputs:
- new_state: float32 [9, 20, 147456], P(None, None, 'dom')
Inputs may be any that keep to these rules, and one draw needn't show every extreme that they name: `element_new_slot`: one to one into slots partition * 1152 + local slot. Element 896 + j of partition d either stays at its local index or, on partitions that shed work, goes with g = j div 16 to partition (d + max(g * 16, 1)) mod 128, local slot 1024 + g * 16 + j mod 16; a partition sheds all 128 such elements or none; elements below 896 stay. Partitions 0 and 127 receive all 8 groups. `neighbours`: each names an occupied slot whose local index is below 896, on the element's own partition after migration or on one at s partitions' distance, s in -4..4 or s = 64, cyclically; at most one face of an element lies off its partition; from the elements of one partition after migration at most 32 faces name any one other partition, and partition 0 is named by exactly 32 faces from each of the nine partitions at those distances.
All inputs are finite; a program needn't handle non-finite values. No bound on the sum of `element_cluster_index` on one device may be relied on, other than what follows from the above.
Results may differ from a plain program's by a relative error of at most 0.0001.
Values sent between devices are 32-bit elements; how exact they have to be, the bound alone decides.
A program may use at most 256 MiB of HBM per device.

v0:
```python
import math

import jax
import jax.numpy as jnp
from jax import lax
from jax.sharding import PartitionSpec as P

NORDER = 4
CSZ = 16
PARTITION_SLOTS = 1152
REQ = 32


step_fast = 0.25
precise = lax.Precision.HIGHEST


def coefficients(lower, upper):
    return [
        (upper ** (degree + 1) - lower ** (degree + 1)) / math.factorial(degree + 1)
        for degree in range(NORDER)
    ]


def jacobian_apply(element_jacobian_set, turned):
    return jnp.sum(element_jacobian_set[:, :, :, None, :] * turned[:, None, :, :, :], axis=(0, 2))


def predictor(present_state, element_jacobian_set, deriv_mats):
    series = [present_state]
    for degree in range(NORDER - 1):
        turned = jnp.einsum("qce,dcb->dqbe", series[-1], deriv_mats, precision=precise)
        series.append(-jacobian_apply(element_jacobian_set, turned))
    return series


def integrate(series, lower, upper):
    result = jnp.zeros_like(series[0])
    for factor, member in zip(coefficients(lower, upper), series):
        result = result + factor * member
    return result


def update(
    integral,
    outside,
    element_jacobian_set,
    scaled_normals,
    element_speeds,
    face_tables,
    stiff_mats,
    face_eval,
    face_lift,
):
    turned = jnp.einsum("qce,dcb->dqbe", integral, stiff_mats, precision=precise)
    change = jacobian_apply(element_jacobian_set, turned)
    for which_face in range(4):
        inner = jnp.einsum("pbe,bn->pne", integral, face_eval[3 * which_face], precision=precise)
        outer = jnp.sum(outside[which_face][:, :, None, :] * face_tables[which_face][None], axis=1)
        normal_star = jnp.sum(
            scaled_normals[which_face][:, None, None, :] * element_jacobian_set, axis=0
        )
        mixed_flux = jnp.sum(normal_star[:, :, None, :] * (inner + outer)[None], axis=1)
        flux = 0.5 * mixed_flux + 0.5 * element_speeds * (inner - outer)
        change = change - jnp.einsum("pne,nb->pbe", flux, face_lift[which_face], precision=precise)
    return change


def per_device(
    element_freedom_values,
    scaled_jacobian_matrices,
    outward_face_normals,
    largest_wave_speed,
    element_cluster_index,
    element_new_slot,
    neighbours,
    face_rotation_codes,
    deriv_mats,
    stiff_mats,
    face_eval,
    face_lift,
):
    nvar, nbasis, count = element_freedom_values.shape
    width = nvar * nbasis
    devices = lax.axis_size("dom")
    myself = lax.axis_index("dom")
    floats = jnp.concatenate(
        [
            element_freedom_values.reshape(width, count),
            scaled_jacobian_matrices.reshape(-1, count),
            outward_face_normals.reshape(-1, count),
            largest_wave_speed[None, :],
            jnp.ones((1, count), jnp.float32),
        ],
        axis=0,
    )
    target = element_new_slot // PARTITION_SLOTS
    local_slot = element_new_slot % PARTITION_SLOTS
    leaving = target != myself
    integers = jnp.concatenate(
        [
            element_cluster_index[None, :],
            neighbours,
            face_rotation_codes,
            (local_slot + 1)[None, :],
        ],
        axis=0,
    )
    float_rows = floats.shape[0]
    int_rows = integers.shape[0]
    peers = ((target[:, None] == jnp.arange(devices)[None, :]) & leaving[:, None]).astype(jnp.int32)
    ranks = jnp.sum((jnp.cumsum(peers, axis=0) - 1) * peers, axis=1)
    length = devices * CSZ
    where_to = jnp.where(leaving, target * CSZ + ranks, length)
    send_f = (
        jnp.zeros((float_rows, length + 1), jnp.float32).at[:, where_to].set(floats)[:, :length]
    )
    send_i = jnp.zeros((int_rows, length + 1), jnp.int32).at[:, where_to].set(integers)[:, :length]
    send_f, send_i = (send_f, send_i)
    got_f, got_i = (
        lax.all_to_all(
            send_f.reshape(float_rows, devices, CSZ), "dom", split_axis=1, concat_axis=1, tiled=True
        ),
        lax.all_to_all(
            send_i.reshape(int_rows, devices, CSZ), "dom", split_axis=1, concat_axis=1, tiled=True
        ),
    )
    arrive_f = got_f.reshape(float_rows, -1)
    arrive_i = got_i.reshape(int_rows, -1)
    staying = jnp.where(leaving, PARTITION_SLOTS, local_slot)
    arrival = arrive_i[-1] - 1
    landing = jnp.where(arrival >= 0, arrival, PARTITION_SLOTS)
    placed_f = (
        jnp.zeros((float_rows, PARTITION_SLOTS + 1), jnp.float32)
        .at[:, staying]
        .set(floats)
        .at[:, landing]
        .set(arrive_f)[:, :PARTITION_SLOTS]
    )
    placed_i = (
        jnp.zeros((int_rows, PARTITION_SLOTS + 1), jnp.int32)
        .at[:, staying]
        .set(integers)
        .at[:, landing]
        .set(arrive_i)[:, :PARTITION_SLOTS]
    )
    present_state = placed_f[:width].reshape(nvar, nbasis, PARTITION_SLOTS)
    offset_star = width + 3 * nvar * nvar
    element_jacobian_set = placed_f[width:offset_star].reshape(3, nvar, nvar, PARTITION_SLOTS)
    scaled_normals = placed_f[offset_star : offset_star + 12].reshape(4, 3, PARTITION_SLOTS)
    element_speeds = placed_f[offset_star + 12]
    occupied = placed_f[offset_star + 13]
    time_clusters = placed_i[0]
    neighbour_links = placed_i[1:5]
    face_rotations = placed_i[5:9]
    face_tables = jnp.transpose(jnp.take(face_eval, face_rotations, axis=0), (0, 2, 3, 1))
    owner = (neighbour_links // PARTITION_SLOTS).reshape(-1)
    spot_local = (neighbour_links % PARTITION_SLOTS).reshape(-1)
    remote = (owner != myself) & (jnp.tile(occupied, 4) > 0)
    peers = ((owner[:, None] == jnp.arange(devices)[None, :]) & remote[:, None]).astype(jnp.int32)
    ranks = jnp.sum((jnp.cumsum(peers, axis=0) - 1) * peers, axis=1)
    length = devices * REQ
    where_at = jnp.where(remote, owner * REQ + ranks, length)
    asks = (
        jnp.zeros((length + 1,), jnp.int32)
        .at[where_at]
        .set(spot_local + 1)[:length]
        .reshape(devices, REQ)
    )
    wanted = lax.all_to_all(asks, "dom", split_axis=0, concat_axis=0, tiled=True)

    def fetch_remote(flattened):
        picked = flattened[:, jnp.maximum(wanted - 1, 0)]
        returned = lax.all_to_all(picked, "dom", split_axis=1, concat_axis=1, tiled=True)
        return returned.reshape(width, -1)

    read_at = jnp.minimum(where_at, length - 1)

    def outside(data):
        flattened = data.reshape(width, PARTITION_SLOTS)
        joined = jnp.where(
            remote[None, :], fetch_remote(flattened)[:, read_at], flattened[:, spot_local]
        )
        joined = joined.reshape(nvar, nbasis, 4, PARTITION_SLOTS)
        return [joined[:, :, which_face] for which_face in range(4)]

    def apply(integral, others):
        return update(
            integral,
            others,
            element_jacobian_set,
            scaled_normals,
            element_speeds,
            face_tables,
            stiff_mats,
            face_eval,
            face_lift,
        )

    fast = (time_clusters == 0)[None, None, :]
    series = predictor(present_state, element_jacobian_set, deriv_mats)
    first = integrate(series, 0.0, step_fast)
    slow_second = integrate(series, step_fast, 2.0 * step_fast)
    first_out = outside(first)
    midway = jnp.where(fast, present_state + apply(first, first_out), present_state)
    fast_second = integrate(predictor(midway, element_jacobian_set, deriv_mats), 0.0, step_fast)
    second = jnp.where(fast, fast_second, slow_second)
    second_out = outside(second)
    fast_end = midway + apply(second, second_out)
    total = first + second
    total_out = [first_out[which_face] + second_out[which_face] for which_face in range(4)]
    slow_end = present_state + apply(total, total_out)
    return jnp.where(fast, fast_end, slow_end)


def solution(mesh):
    placed = (
        P(None, None, "dom"),
        P(None, None, None, "dom"),
        P(None, None, "dom"),
        P("dom"),
        P("dom"),
        P("dom"),
        P(None, "dom"),
        P(None, "dom"),
        P(),
        P(),
        P(),
        P(),
    )
    return jax.shard_map(
        per_device, mesh=mesh, in_specs=placed, out_specs=P(None, None, "dom"), check_vma=False
    )
```

profile of v0, /device:TPU:1, one launch (start us, length us, event | category | flops | bytes accessed | tf_op | source)
XLA Modules:
  0.0 573.5 jit_solution(8352994070697044370)
XLA Ops:
  8.5 12.0 %all-to-all-start = ((s32[128,1,160]{2,1,0:T(1,128)}), s32[128,1,160]{2,1,0:T(1,128)}, u32[]{:S(2)}, u32[]{:S(2)}) async-start(s32[128,1,160]{2,1,0:T(1,128)} %reshape.577), calls=%async_computation | async-start | bytes 262144 | tf_op jit(solution)/shard_map/all_to_all | solution.py:124
  28.1 7.6 %scatter_custom_fusion.4 = f32[437,2049]{0,1:T(8,128)} fusion(s32[1024]{0:T(1024)S(1)} %compare_select_fusion.6, f32[1024,437]{1,0:T(8,128)} %copy.326, f32[]{:T(128)} %constant.43.clone.1), kind=kCustom, calls=%fused_computation.111 | custom fusion | bytes 3582164 | tf_op jit(solution)/shard_map/scatter | solution.py:116
  35.7 6.5 %scatter_custom_fusion.3 = f32[437,1153]{0,1:T(8,128)S(1)} fusion(s32[1024]{0:T(1024)S(1)} %get-tuple-element.33, f32[1024,437]{1,0:T(8,128)} %copy.326, f32[]{:T(128)} %constant.43.clone.1), kind=kCustom, calls=%fused_computation.121 | custom fusion | bytes 2015956 | tf_op jit(solution)/shard_map/scatter | solution.py:136
  45.8 4.6 slice.227
  50.4 10.2 %all-to-all-start.1 = ((f32[437,128,16]{0,2,1:T(8,128)}), f32[437,128,16]{0,2,1:T(8,128)}, u32[]{:S(2)}, u32[]{:S(2)}) async-start(f32[437,128,16]{0,2,1:T(8,128)} %bitcast.389), calls=%async_computation.1 | async-start | bytes 8388608 | tf_op jit(solution)/shard_map/all_to_all | solution.py:121
  70.8 6.1 %scatter_fusion = s32[10,1153]{0,1:T(8,128)S(1)} fusion(s32[10,1153]{0,1:T(8,128)S(1)} %scatter_custom_fusion, s32[2048]{0:T(1024)S(1)} %bitcast.414, s32[2048,10]{1,0:T(8,128)} %copy.323), kind=kCustom, calls=%fused_computation.9 | custom fusion | bytes 253952 | tf_op jit(solution)/shard_map/scatter | solution.py:145
  83.1 15.2 %gather_fusion.3 = f32[4608,20,16]{1,2,0:T(8,128)} fusion(f32[12,20,16]{1,2,0:T(8,128)S(1)} %copy-done.1, s32[5120]{0:T(1024)S(1)} %pad_clamp_fusion), kind=kCustom, calls=%fused_computation.3 | custom fusion | bytes 11814912 | tf_op jit(solution)/shard_map/jit(_take)/gather | solution.py:156
  98.3 25.5 %select_bitcast_fusion = f32[4,20,16,1152]{1,2,3,0:T(8,128)} fusion(f32[4,1152,20,16]{2,3,1,0:T(8,128)} %bitcast.384, pred[4,1152]{1,0:T(4,128)(4,1)S(1)} %compare_and_fusion.2), kind=kLoop, calls=%fused_computation.14 | loop fusion | flops 1474560 | bytes 11801088 | tf_op jit(solution)/shard_map/jit(_take)/select_n | solution.py:156
  123.8 10.5 %scatter_fusion.1 = f32[437,1153]{0,1:T(8,128)S(1)} fusion(f32[437,1153]{0,1:T(8,128)S(1)} %scatter_custom_fusion.3, s32[2048]{0:T(1024)S(1)} %bitcast.415, f32[2048,437]{1,0:T(8,128)} %bitcast.15), kind=kCustom, calls=%fused_computation.12 | custom fusion | bytes 10747904 | tf_op jit(solution)/shard_map/scatter | solution.py:138
  147.9 6.1 %convolution_bitcast_fusion.8 = f32[3,9,20,1152]{3,2,0,1:T(8,128)} fusion(f32[9,20,1152,1]{2,1,0,3:T(8,128)} %reshape.521, f32[3,20,20]{2,1,0:T(8,128)S(1)} %copy-done), kind=kOutput, calls=%fused_computation.60 | convolution fusion | flops 149299200 | bytes 3322560 | tf_op jit(solution)/shard_map/qce,dcb->dqbe/dot_general | solution.py:32
  154.0 4.3 multiply_reduce_fusion.8
  162.5 4.3 multiply_reduce_fusion.7
  170.9 4.7 multiply_reduce_fusion.6
  188.1 17.6 %scatter_custom_fusion.6 = s32[4097]{0:T(1024)S(1)} fusion(s32[4608]{0:T(1024)S(1)} %get-tuple-element.28, s32[4608]{0:T(1024)} %reshape.507, s32[]{:T(128)} %constant.34.clone.1), kind=kCustom, calls=%fused_computation.286 | custom fusion | bytes 16900 | tf_op jit(solution)/shard_map/scatter | solution.py:167
  206.4 9.8 %all-to-all-start.2 = ((s32[128,1,32]{2,1,0:T(1,128)}), s32[128,1,32]{2,1,0:T(1,128)S(1)}, u32[]{:S(2)}, u32[]{:S(2)}) async-start(s32[128,1,32]{2,1,0:T(1,128)} %bitcast.37), calls=%async_computation.2 | async-start | bytes 131072 | tf_op jit(solution)/shard_map/all_to_all | solution.py:170
  218.4 7.2 %all-to-all-done.2 = s32[128,1,32]{2,1,0:T(1,128)S(1)} async-done(((s32[128,1,32]{2,1,0:T(1,128)}), s32[128,1,32]{2,1,0:T(1,128)S(1)}, u32[]{:S(2)}, u32[]{:S(2)}) %all-to-all-start.2) | async-done | bytes 16416 | tf_op jit(solution)/shard_map/all_to_all | solution.py:170
  226.0 16.1 %gather_fusion = f32[4096,180]{1,0:T(8,128)} fusion(f32[180,1152]{0,1:T(8,128)S(1)} %copy.344, s32[4096]{0:T(1024)S(1)} %broadcast_clamp_fusion), kind=kCustom, calls=%fused_computation | custom fusion | bytes 5914624 | tf_op jit(solution)/shard_map/gather | solution.py:173
  242.1 5.4 all-to-all-start.3
  247.5 25.4 %slice_bitcast_fusion = (f32[20,16,1152]{0,1,2:T(8,128)}, f32[20,16,1152]{0,1,2:T(8,128)}, f32[20,16,1152]{0,1,2:T(8,128)}, f32[20,16,1152]{0,1,2:T(8,128)}) fusion(f32[4,20,16,1152]{1,2,3,0:T(8,128)} %select_bitcast_fusion), kind=kLoop, calls=%fused_computation.36 | loop fusion | bytes 11796480 | tf_op jit(solution)/shard_map/mul | solution.py:59
  272.9 6.9 %copy.349 = f32[20,16,1152]{2,1,0:T(8,128)} copy(f32[20,16,1152]{0,1,2:T(8,128)} %get-tuple-element.39) | data formatting | bytes 2949120 | tf_op jit(solution)/shard_map/mul | solution.py:59
  279.8 6.9 %copy.351 = f32[20,16,1152]{2,1,0:T(8,128)} copy(f32[20,16,1152]{0,1,2:T(8,128)} %get-tuple-element.38) | data formatting | bytes 2949120 | tf_op jit(solution)/shard_map/mul | solution.py:59
  286.7 6.9 %copy.353 = f32[20,16,1152]{2,1,0:T(8,128)} copy(f32[20,16,1152]{0,1,2:T(8,128)} %get-tuple-element.37) | data formatting | bytes 2949120 | tf_op jit(solution)/shard_map/mul | solution.py:59
  293.6 6.9 %copy.355 = f32[20,16,1152]{2,1,0:T(8,128)} copy(f32[20,16,1152]{0,1,2:T(8,128)} %get-tuple-element.36) | data formatting | bytes 2949120 | tf_op jit(solution)/shard_map/mul | solution.py:59
  302.7 11.8 %gather_fusion.2 = f32[4608,180]{1,0:T(8,128)} fusion(f32[180,1152]{0,1:T(8,128)S(1)} %copy.344, s32[5120]{0:T(1024)S(1)} %pad_clamp_fusion.1), kind=kCustom, calls=%fused_computation.2 | custom fusion | bytes 6653952 | tf_op jit(solution)/shard_map/gather | solution.py:182
  314.5 5.6 copy.347
  320.1 5.4 gather.34
  335.5 4.2 multiply_reduce_fusion.33
  345.7 14.0 %gather_fusion.1 = f32[4608,180]{1,0:T(8,128)} fusion(f32[180,4096]{0,1:T(8,128)} %bitcast.40, s32[5120]{0:T(1024)S(1)} %pad_clamp_fusion.2), kind=kCustom, calls=%fused_computation.1 | custom fusion | bytes 6653952 | tf_op jit(solution)/shard_map/gather | solution.py:182
  359.6 5.6 copy.345
  365.2 5.1 gather.32
  392.1 4.2 convolution_bitcast_fusion.4
  396.2 4.3 multiply_reduce_fusion.4
  400.6 4.2 convolution_bitcast_fusion.3
  404.7 4.3 multiply_reduce_fusion.3
  410.0 4.4 convolution_bitcast_fusion.2
  414.4 5.4 multiply_reduce_fusion.2
  419.7 4.4 fusion.208
  427.7 16.1 %gather_fusion.4 = f32[4096,180]{1,0:T(8,128)} fusion(f32[180,1152]{0,1:T(8,128)S(1)} %copy.364, s32[4096]{0:T(1024)S(1)} %broadcast_clamp_fusion), kind=kCustom, calls=%fused_computation.4 | custom fusion | bytes 5914624 | tf_op jit(solution)/shard_map/gather | solution.py:173
  443.7 10.4 %all-to-all-start.4 = ((f32[180,128,32]{0,2,1:T(8,128)}), f32[180,128,32]{0,2,1:T(8,128)}, u32[]{:S(2)}, u32[]{:S(2)}) async-start(f32[180,128,32]{0,2,1:T(8,128)} %bitcast.386), calls=%async_computation.4 | async-start | bytes 8388608 | tf_op jit(solution)/shard_map/all_to_all | solution.py:174
  454.1 11.8 %gather_fusion.6 = f32[4608,180]{1,0:T(8,128)} fusion(f32[180,1152]{0,1:T(8,128)S(1)} %copy.364, s32[5120]{0:T(1024)S(1)} %pad_clamp_fusion.1), kind=kCustom, calls=%fused_computation.6 | custom fusion | bytes 6653952 | tf_op jit(solution)/shard_map/gather | solution.py:182
  465.9 5.6 copy.367
  471.5 5.2 gather.40
  485.0 8.9 %multiply_reduce_fusion = (f32[9,20,1152]{2,1,0:T(8,128)}, f32[9,20,1152]{2,1,0:T(8,128)}) fusion(f32[3,9,9,1152]{3,2,1,0:T(8,128)S(1)} %copy-done.6, f32[3,9,20,1152]{3,2,0,1:T(8,128)} %convolution_bitcast_fusion.1, f32[3,9,20,1152]{3,2,0,1:T(8,128)} %convolution_bitcast_fusion), kind=kLoop, calls=%fused_computation.15 | loop fusion | flops 21980160 | bytes 7755264 | tf_op jit(solution)/shard_map/reduce_sum | solution.py:26
  493.9 12.9 %all-to-all-done.4 = f32[180,128,32]{0,2,1:T(8,128)} async-done(((f32[180,128,32]{0,2,1:T(8,128)}), f32[180,128,32]{0,2,1:T(8,128)}, u32[]{:S(2)}, u32[]{:S(2)}) %all-to-all-start.4) | async-done | bytes 2949152 | tf_op jit(solution)/shard_map/all_to_all | solution.py:174
  506.7 14.0 %gather_fusion.5 = f32[4608,180]{1,0:T(8,128)} fusion(f32[180,4096]{0,1:T(8,128)} %bitcast.89, s32[5120]{0:T(1024)S(1)} %pad_clamp_fusion.2), kind=kCustom, calls=%fused_computation.5 | custom fusion | bytes 6653952 | tf_op jit(solution)/shard_map/gather | solution.py:182
  520.7 5.9 %copy.365 = f32[180,4608]{1,0:T(8,128)} copy(f32[180,4608]{0,1:T(8,128)} %bitcast.391) | data formatting | bytes 6635520 | tf_op jit(solution)/shard_map/gather | solution.py:182
  526.7 5.1 gather.38
  535.7 4.7 slice_add_fusion.1
  (284 shorter events, 162.0 us)
Async XLA Ops:
  0.0 147.9 %copy-start = (f32[3,20,20]{2,1,0:T(8,128)S(1)}, f32[3,20,20]{2,1,0:T(8,128)}, u32[]{:S(2)}) copy-start(f32[3,20,20]{2,1,0:T(8,128)} %param.20) | copy-start | bytes 14404
  0.0 2.1 copy-start.57
  0.0 2.1 copy-start.58
  0.0 2.1 copy-start.60
  6.5 16.1 %copy-start.49 = (f32[3,9,9,1024]{3,0,2,1:T(4,128)S(1)}, f32[3,9,9,1024]{3,0,2,1:T(4,128)}, u32[]{:S(2)}) copy-start(f32[3,9,9,1024]{3,0,2,1:T(4,128)} %param.13) | copy-start | bytes 2985988
  8.5 41.9 %all-to-all-start = ((s32[128,1,160]{2,1,0:T(1,128)}), s32[128,1,160]{2,1,0:T(1,128)}, u32[]{:S(2)}, u32[]{:S(2)}) async-start(s32[128,1,160]{2,1,0:T(1,128)} %reshape.577), calls=%async_computation | async-start | bytes 262144 | tf_op jit(solution)/shard_map/all_to_all | solution.py:124
  50.4 73.3 %all-to-all-start.1 = ((f32[437,128,16]{0,2,1:T(8,128)}), f32[437,128,16]{0,2,1:T(8,128)}, u32[]{:S(2)}, u32[]{:S(2)}) async-start(f32[437,128,16]{0,2,1:T(8,128)} %bitcast.389), calls=%async_computation.1 | async-start | bytes 8388608 | tf_op jit(solution)/shard_map/all_to_all | solution.py:121
  70.8 12.2 %copy-start.1 = (f32[12,20,16]{1,2,0:T(8,128)S(1)}, f32[12,20,16]{1,2,0:T(8,128)}, u32[]{:S(2)}) copy-start(f32[12,20,16]{1,2,0:T(8,128)} %param.22) | copy-start | bytes 46084
  77.0 21.3 %copy-start.16 = (s32[10,1153]{0,1:T(8,128)}, s32[10,1153]{0,1:T(8,128)S(1)}, u32[]{:S(2)}) copy-start(s32[10,1153]{0,1:T(8,128)S(1)} %scatter_fusion) | copy-start | bytes 138364
  134.3 9.0 %copy-start.3 = (f32[437,1153]{0,1:T(8,128)}, f32[437,1153]{0,1:T(8,128)S(1)}, u32[]{:S(2)}) copy-start(f32[437,1153]{0,1:T(8,128)S(1)} %scatter_fusion.1) | copy-start | bytes 6046336
  140.7 34.9 %copy-start.13 = (f32[9,20,1152]{2,1,0:T(8,128)}, f32[9,20,1152]{2,1,0:T(8,128)S(1)}, u32[]{:S(2)}) copy-start(f32[9,20,1152]{2,1,0:T(8,128)S(1)} %reshape.393) | copy-start | bytes 2488324
  147.9 23.0 %copy-start.5 = (f32[3,9,9,1152]{3,2,1,0:T(8,128)}, f32[3,9,9,1152]{3,2,1,0:T(8,128)S(1)}, u32[]{:S(2)}) copy-start(f32[3,9,9,1152]{3,2,1,0:T(8,128)S(1)} %mul.347) | copy-start | bytes 3359236
  158.3 17.3 %copy-start.18 = (f32[9,20,1152]{2,1,0:T(8,128)}, f32[9,20,1152]{2,1,0:T(8,128)S(1)}, u32[]{:S(2)}) copy-start(f32[9,20,1152]{2,1,0:T(8,128)S(1)} %multiply_reduce_fusion.8) | copy-start | bytes 2488324
  166.8 8.9 %copy-start.20 = (f32[9,20,1152]{2,1,0:T(8,128)}, f32[9,20,1152]{2,1,0:T(8,128)S(1)}, u32[]{:S(2)}) copy-start(f32[9,20,1152]{2,1,0:T(8,128)S(1)} %multiply_reduce_fusion.7) | copy-start | bytes 2488324
  183.5 4.5 copy-start.54
  183.5 32.7 %copy-start.24 = (f32[180,1152]{1,0:T(8,128)S(1)}, f32[180,1152]{1,0:T(8,128)}, u32[]{:S(2)}) copy-start(f32[180,1152]{1,0:T(8,128)} %copy.410) | copy-start | bytes 2488324
  206.4 19.3 %all-to-all-start.2 = ((s32[128,1,32]{2,1,0:T(1,128)}), s32[128,1,32]{2,1,0:T(1,128)S(1)}, u32[]{:S(2)}, u32[]{:S(2)}) async-start(s32[128,1,32]{2,1,0:T(1,128)} %bitcast.37), calls=%async_computation.2 | async-start | bytes 131072 | tf_op jit(solution)/shard_map/all_to_all | solution.py:170
  218.0 24.0 %copy-start.37 = (f32[180,1152]{1,0:T(8,128)}, f32[180,1152]{1,0:T(8,128)S(1)}, u32[]{:S(2)}) copy-start(f32[180,1152]{1,0:T(8,128)S(1)} %add_add_fusion.2) | copy-start | bytes 2488324
  242.1 103.6 %all-to-all-start.3 = ((f32[180,128,32]{0,2,1:T(8,128)}), f32[180,128,32]{0,2,1:T(8,128)}, u32[]{:S(2)}, u32[]{:S(2)}) async-start(f32[180,128,32]{0,2,1:T(8,128)} %bitcast.385), calls=%async_computation.3 | async-start | bytes 8388608 | tf_op jit(solution)/shard_map/all_to_all | solution.py:174
  272.9 6.9 %copy-start.53 = (s32[1,1,4,1152]{3,2,1,0:T(4,128)S(1)}, s32[1,1,4,1152]{3,2,1,0:T(4,128)}, u32[]{:S(2)}) copy-start(s32[1,1,4,1152]{3,2,1,0:T(4,128)} %get-tuple-element.62) | copy-start | bytes 55300
  293.6 7.0 %copy-start.17 = (s32[10,1153]{0,1:T(8,128)S(1)}, s32[10,1153]{0,1:T(8,128)}, u32[]{:S(2)}) copy-start(s32[10,1153]{0,1:T(8,128)} %copy-done.16) | copy-start | bytes 138364
  320.1 5.4 copy-start.4
  331.3 8.4 %copy-start.51 = (f32[3,20,20]{2,1,0:T(8,128)S(1)}, f32[3,20,20]{2,1,0:T(8,128)}, u32[]{:S(2)}) copy-start(f32[3,20,20]{2,1,0:T(8,128)} %param.21) | copy-start | bytes 14404
  335.1 4.7 copy-start.34
  335.5 6.8 %copy-start.6 = (f32[3,9,9,1152]{3,2,1,0:T(8,128)S(1)}, f32[3,9,9,1152]{3,2,1,0:T(8,128)}, u32[]{:S(2)}) copy-start(f32[3,9,9,1152]{3,2,1,0:T(8,128)} %copy-done.5) | copy-start | bytes 3359236
  373.6 2.7 copy-start.11
  376.3 2.4 copy-start.2
  376.5 2.9 copy-start.29
  381.5 2.2 copy-start.25
  383.7 1.8 copy-start.44
  383.7 2.3 copy-start.42
  384.7 1.7 copy-start.40
  388.4 2.5 copy-start.14
  388.4 2.5 copy-start.56
  392.1 8.5 %copy-start.22 = (f32[9,20,1152]{2,1,0:T(8,128)}, f32[9,20,1152]{2,1,0:T(8,128)S(1)}, u32[]{:S(2)}) copy-start(f32[9,20,1152]{2,1,0:T(8,128)S(1)} %fusion.13) | copy-start | bytes 2488324
  400.5 8.5 %copy-start.35 = (f32[9,20,1152]{2,1,0:T(8,128)}, f32[9,20,1152]{2,1,0:T(8,128)S(1)}, u32[]{:S(2)}) copy-start(f32[9,20,1152]{2,1,0:T(8,128)S(1)} %multiply_reduce_fusion.4) | copy-start | bytes 2488324
  414.4 5.4 copy-start.19
  414.4 5.4 copy-start.21
  443.7 63.0 %all-to-all-start.4 = ((f32[180,128,32]{0,2,1:T(8,128)}), f32[180,128,32]{0,2,1:T(8,128)}, u32[]{:S(2)}, u32[]{:S(2)}) async-start(f32[180,128,32]{0,2,1:T(8,128)} %bitcast.386), calls=%async_computation.4 | async-start | bytes 8388608 | tf_op jit(solution)/shard_map/all_to_all | solution.py:174
  471.5 5.2 copy-start.8
  476.7 4.1 copy-start.9
  531.8 3.9 copy-start.12
  541.8 3.3 copy-start.10
  560.3 1.8 copy-start.41
  561.2 1.7 copy-start.39
  562.0 1.7 copy-start.47
  564.8 2.1 copy-start.23
  569.2 2.1 copy-start.15
  (18 other events, 23.0 us)
where the time goes:
time: 584 us; the launch traced here: 574 us
  local copies, waits for them, and re-layouts  322 us (55%)
  other arithmetic  122 us (21%)
  matrix products  61 us (10%)
  starting transfers between devices  47.7 us (8%)
  waiting for transfers between devices  20.1 us (3%)
    mul x5, local copies, waits for them, and re-layouts, update(): outside[which_face][:, :, None, :] * face_tables[which_face][None]  53 us
    gather x6, local copies, waits for them, and re-layouts, outside(): fetch_remote(flattened)[:, read_at]  49.7 us
    gather x6, local copies, waits for them, and re-layouts, outside(): flattened[:, spot_local]  45.4 us
    reduce_sum x8, other arithmetic, jacobian_apply(): jnp.sum(element_jacobian_set[:, :, :, None, :] * turned[:, None, :, :, :]...  39.5 us
    gather x2, local copies, waits for them, and re-layouts, fetch_remote(): picked = flattened[:, jnp.maximum(wanted - 1, 0)]  32.2 us
    dot_general x6, matrix products, predictor(): jnp.einsum('qce,dcb->dqbe', series[-1], deriv_mats, precision=precise)  27 us
    select_n x2, other arithmetic, per_device(): jnp.take(face_eval, face_rotations, axis=0)  25.5 us
    scatter x1, local copies, waits for them, and re-layouts, per_device(): asks = jnp.zeros((length + 1,), jnp.int32).at[where_at].set(spot_local +...  17.6 us
  transfers between devices with their start and end apart: 5, of which 2 were waited for; matrix products, arithmetic and copies ran while one was open for 41% of the time, Pallas kernels for 0%

commit v1 on v0

v1 whole, which is shorter than its diff:
```python
import functools
import math

import jax
import jax.numpy as jnp
import numpy as np
from jax import lax
from jax.experimental import pallas as pl
from jax.experimental.pallas import tpu as pltpu
from jax.sharding import PartitionSpec as P

NORDER = 4
CSZ = 16
GROUPS = 8
E_DEV = 1024
KEEP = 896
PARTITION_SLOTS = 1152
REQ = 32
NQ = 16
QN = 9
BN = 20
LANES = 128
BLOCKS = PARTITION_SLOTS // LANES
KEPT_BLOCKS = KEEP // LANES
ROWS = 184
TAIL = 144
SLAB = 512
ASKS = 384
STEP = 0.25
F32 = jnp.float32
BF16 = jnp.bfloat16
MESH = pl.DeviceIdType.MESH


def coefficients(lower, upper):
    return [
        (upper ** (degree + 1) - lower ** (degree + 1)) / math.factorial(degree + 1)
        for degree in range(NORDER)
    ]


def halves(matrix):
    high = lax.reduce_precision(matrix, 8, 7)
    return high.astype(BF16), (matrix - high).astype(BF16)


def stacked(matrix):
    high, low = halves(matrix)
    return jnp.concatenate([high, high, low], axis=-1)


DUP = np.array(list(range(20)) + [16, 17, 18, 19])


def grouped(mats, many):
    turned = jnp.swapaxes(mats, 1, 2)[:, DUP, :]
    eye = jnp.eye(many, dtype=F32)
    blown = turned[:, None, :, None, :] * eye[None, :, None, :, None]
    rows = mats.shape[0] * many * 24
    main = blown[..., :16].reshape(rows, many * 16)
    tail = blown[..., 16:].reshape(rows, many * 4)
    parts = [main, tail]
    if many == 1:
        parts.append(jnp.zeros((rows, 12), F32))
    return jnp.concatenate(parts, axis=1)


def grouped_points(mats, many):
    turned = jnp.swapaxes(mats, 1, 2)[:, DUP, :]
    eye = jnp.eye(many, dtype=F32)
    blown = turned[:, None, :, None, :] * eye[None, :, None, :, None]
    return blown.reshape(mats.shape[0], many * 24, many * NQ)


def constants(deriv_mats, stiff_mats, face_eval, face_lift):
    own = jnp.einsum("fcn,fnb->fcb", face_eval[::3], face_lift, precision=lax.Precision.HIGHEST)
    full = jnp.concatenate([stiff_mats, jnp.sum(own, axis=0)[None]], axis=0)
    result = []
    for many in (4, 1):
        result.append(stacked(grouped(-deriv_mats, many)))
    for many in (4, 1):
        result.append(stacked(grouped(full, many)))
    for many in (4, 1):
        inside = stacked(grouped(0.5 * own, many)).reshape(4, many * 24, -1)
        beyond = stacked(grouped_points(0.5 * face_lift, many))
        result.append(jnp.concatenate([inside, beyond], axis=-1))
    table = jnp.pad(face_eval.reshape(12, BN * NQ).T, ((0, 0), (0, 4)))
    result.append(jnp.concatenate(halves(table), axis=1))
    return result


def dot(a, b):
    return jnp.dot(a, b, preferred_element_type=F32)


def dot_nt(a, b):
    return lax.dot_general(a, b, (((1,), (1,)), ((), ())), preferred_element_type=F32)


def split(value):
    high = value.astype(BF16)
    return high, (value - high.astype(F32)).astype(BF16)


def triple(value):
    high, low = split(value)
    return jnp.concatenate([high, low, high], axis=0)


def lanes_of(ref, first, many, start, size):
    parts = [ref[first + i, pl.ds(start, size), :] for i in range(many)]
    return parts[0] if many == 1 else jnp.concatenate(parts, axis=1)


def quad_rows(ref, first, many, group):
    if group < 2:
        main = lanes_of(ref, first, many, 64 * group, 64)
        tail = lanes_of(ref, first, many, TAIL + 16 * group, 16)
        return triple(jnp.concatenate([main, tail], axis=0))
    main = lanes_of(ref, first, many, 128, 16)
    tail = lanes_of(ref, first, many, TAIL + 32, 8)
    blank = jnp.zeros((8, main.shape[1]), F32)
    return triple(jnp.concatenate([main, tail, blank], axis=0))


def put(ref, first, many, start, value):
    for i in range(many):
        ref[first + i, pl.ds(start, value.shape[0]), :] = value[:, LANES * i : LANES * (i + 1)]


def in_pairs(body, blocks):
    def step(i, carry):
        body(2 * i, 2)
        return carry

    lax.fori_loop(0, blocks // 2, step, 0)
    if blocks % 2:
        body(blocks - 1, 1)


def kernel(
    count,
    x_ref,
    jac_hbm,
    normal_ref,
    speed_ref,
    cluster_ref,
    slot_ref,
    link_ref,
    turn_ref,
    pred4_ref,
    pred1_ref,
    stiff4_ref,
    stiff1_ref,
    face4_ref,
    face1_ref,
    table_ref,
    out_ref,
    jac,
    pairs,
    info,
    present,
    first,
    second,
    base,
    series,
    turned,
    faces,
    points,
    gathered,
    tables,
    sources,
    wanted,
    placed,
    arrived,
    pack,
    got,
    ask_out,
    ask_in,
    answer_out,
    answer_in,
    jac_sem,
    pack_send,
    pack_recv,
    ask_send,
    ask_recv,
    answer_send,
    answer_recv,
):
    me = lax.axis_index("dom")
    group_steps = [max(g * (count // GROUPS), 1) for g in range(GROUPS)]
    reach = [1, 2, 3, 4, count - 1, count - 2, count - 3, count - 4, count // 2]
    greeted = sorted(
        {s % count for s in group_steps} | {-s % count for s in group_steps} | {s % count for s in reach}
    )

    def device(step):
        return (lax.rem(me + (step % count), count),)

    barrier = pltpu.get_barrier_semaphore()
    for step in greeted:
        pl.semaphore_signal(barrier, inc=1, device_id=device(step), device_id_type=MESH)

    jac_copy = pltpu.make_async_copy(jac_hbm, jac.at[:, :, :, pl.ds(0, E_DEV)], jac_sem)
    jac_copy.start()

    answer_in[:, pl.ds(288, 96), :] = jnp.zeros((2, 96, 256), F32)

    def load_block(b, carry):
        at = pl.ds(pl.multiple_of(b * LANES, LANES), LANES)
        for q in range(QN):
            present[b, pl.ds(16 * q, 16), :] = x_ref[q, 0:16, at]
            present[b, pl.ds(TAIL + 4 * q, 4), :] = x_ref[q, 16:20, at]
        present[b, pl.ds(180, 4), :] = jnp.zeros((4, LANES), F32)
        for f in range(4):
            info[b, pl.ds(3 * f, 3), :] = normal_ref[f, :, at]
        info[b, pl.ds(12, 1), :] = speed_ref[:, at]
        info[b, pl.ds(13, 1), :] = cluster_ref[:, at].astype(F32)
        info[b, pl.ds(14, 4), :] = link_ref[:, at].astype(F32)
        info[b, pl.ds(18, 4), :] = turn_ref[:, at].astype(F32)
        info[b, pl.ds(22, 2), :] = jnp.ones((2, LANES), F32)
        return carry

    lax.fori_loop(0, 8, load_block, 0)
    lane = lax.broadcasted_iota(jnp.int32, (1, LANES), 1)
    leaves = slot_ref[:, KEEP:E_DEV] != me * PARTITION_SLOTS + KEEP + lane

    jac_copy.wait()
    pack[pl.ds(0, ROWS), :] = jnp.where(leaves, present[7], 0.0)
    pack[pl.ds(ROWS, 24), :] = jnp.where(leaves, info[7], 0.0)
    for d in range(3):
        for p in range(QN):
            pack[pl.ds(208 + 9 * (9 * d + p), 9), :] = jnp.where(
                leaves, jac[d, p, :, pl.ds(KEEP, LANES)], 0.0
            )
    pack[pl.ds(451, SLAB - 451), :] = jnp.zeros((SLAB - 451, LANES), F32)
    for i in range(SLAB // LANES):
        got[0, :, pl.ds(LANES * i, LANES)] = pack[pl.ds(LANES * i, LANES), :].T
    info[7, pl.ds(22, 1), :] = jnp.where(leaves, 0.0, 1.0)

    pl.semaphore_wait(barrier, len(greeted))

    moves = []
    for g, step in enumerate(group_steps):
        part = pl.ds(CSZ * g, CSZ)
        copy = pltpu.make_async_remote_copy(
            src_ref=got.at[0, part],
            dst_ref=got.at[1, part],
            send_sem=pack_send.at[g],
            recv_sem=pack_recv.at[g],
            device_id=device(step),
            device_id_type=MESH,
        )
        copy.start()
        moves.append(copy)

    def pair_block(b, carry):
        at = pl.ds(pl.multiple_of(b * LANES, LANES), LANES)
        low = lax.broadcasted_iota(jnp.int32, (8, LANES), 0) < 4
        for d in range(3):
            for q in range(QN):
                for i in range(5):
                    upper = jac[d, min(2 * i + 1, 8), q : q + 1, at]
                    pairs[b, 9 * d + q, i] = jnp.where(low, jac[d, 2 * i, q : q + 1, at], upper)
        return carry

    def turn(ref, first_block, many, four_ref, one_ref, kinds, target):
        for group in range(3):
            right = quad_rows(ref, first_block, many, group)
            result = dot(four_ref[...] if group < 2 else one_ref[...], right)
            size = 96 if group < 2 else 24
            for d in range(kinds):
                put(target, first_block, many, 216 * d + 96 * group, result[size * d : size * (d + 1)])

    def apply_jacobian(b, load_turned):
        at = pl.ds(pl.multiple_of(b * LANES, LANES), LANES)
        main = None
        tail = None
        for d in range(3):
            for q in range(QN):
                upper, lower = load_turned(d, q)
                column = jac[d, :, q : q + 1, at]
                one = column * upper[None]
                two = pairs[b, 9 * d + q] * lower[None]
                main = one if main is None else main + one
                tail = two if tail is None else tail + two
        return jnp.concatenate([main.reshape(TAIL, LANES), tail.reshape(40, LANES)], axis=0)

    def plain_turned(b):
        def load(d, q):
            value = turned[b, pl.ds(216 * d + 24 * q, 24), :]
            return value[0:16], value[16:24]

        return load

    to_first = coefficients(0.0, STEP)
    to_slow = coefficients(STEP, 2.0 * STEP)

    def predict(start, blocks, from_block, finish):
        for degree in range(NORDER - 1):
            source = start if degree == 0 else series.at[degree - 1]

            def product(b, many):
                turn(source, from_block + b, many, pred4_ref, pred1_ref, 3, turned)

            in_pairs(product, blocks)

            def step(i, carry):
                b = from_block + i
                value = apply_jacobian(b, plain_turned(b))
                if degree < NORDER - 2:
                    series[degree, b] = value
                else:
                    finish(b, [start[b], series[0, b], series[1, b], value])
                return carry

            lax.fori_loop(0, blocks, step, 0)

    def weighted(factors, members):
        total = factors[0] * members[0]
        for factor, member in zip(factors[1:], members[1:]):
            total = total + factor * member
        return total

    def finish_first(b, members):
        first[b] = weighted(to_first, members)
        second[b] = weighted(to_slow, members)

    lax.fori_loop(0, 8, pair_block, 0)
    predict(present, 8, 0, finish_first)

    for copy in moves:
        copy.wait()
    for i in range(SLAB // LANES):
        pack[pl.ds(LANES * i, LANES), :] = got[1, :, pl.ds(LANES * i, LANES)].T
    present[8] = pack[pl.ds(0, ROWS), :]
    info[8] = pack[pl.ds(ROWS, 24), :]
    for d in range(3):
        for p in range(QN):
            jac[d, p, :, pl.ds(E_DEV, LANES)] = pack[pl.ds(208 + 9 * (9 * d + p), 9), :]
    pair_block(8, 0)

    which = lax.broadcasted_iota(jnp.int32, (16, LANES), 0)
    near = jnp.where(which < 4, which + 1, count + 3 - which)
    wanted_step = jnp.where(which < 8, near, jnp.where(which == 8, count // 2, -7)).astype(F32)
    row_f = which.astype(F32)
    me_f = (jnp.zeros((1, LANES), jnp.int32) + me).astype(F32)
    sums = jnp.where(
        lax.broadcasted_iota(jnp.int32, (LANES, 2 * LANES), 0)
        < lax.broadcasted_iota(jnp.int32, (LANES, 2 * LANES), 1),
        1.0,
        0.0,
    ).astype(BF16)

    def owners(b):
        link = info[b, pl.ds(14, 4), :]
        owner = jnp.floor((link + 0.5) * (1.0 / PARTITION_SLOTS))
        local = link - owner * PARTITION_SLOTS
        away = jnp.where(owner != me_f, info[b, pl.ds(22, 1), :], 0.0) > 0.5
        return owner, local, away

    def scan(b, carry):
        running, asked = carry
        owner, local, away = owners(b)
        step = owner - me_f
        step = jnp.where(step < 0.0, step + count, step)
        step = jnp.max(jnp.where(away, step, -1.0), axis=0, keepdims=True)
        spot = jnp.max(jnp.where(away, local, 0.0), axis=0, keepdims=True)
        hit = wanted_step == step
        member = jnp.where(hit, 1.0, 0.0)
        both = dot(member.astype(BF16), sums)
        place = jnp.where(hit, 32.0 * row_f + running + both[:, :LANES], 0.0)
        found = jnp.sum(member, axis=0, keepdims=True)
        place = jnp.sum(place, axis=0, keepdims=True) - (1.0 - found) * 1.0
        high = jnp.floor(spot * 0.125)
        text = jnp.concatenate([high, spot - 8.0 * high, found, jnp.zeros((13, LANES), F32)], axis=0)
        rows = lax.broadcasted_iota(jnp.int32, (ASKS, LANES), 0).astype(F32)
        marks = jnp.where(rows == place, 1.0, 0.0).astype(BF16)
        placed[b] = marks
        asked = asked + dot_nt(text.astype(BF16), marks)
        return running + both[:, LANES:], asked

    _, asked = lax.fori_loop(
        0, BLOCKS, scan, (jnp.zeros((16, LANES), F32), jnp.zeros((16, ASKS), F32))
    )
    asked = jnp.where(asked[2:3] > 0.5, 8.0 * asked[0:1] + asked[1:2], -1.0)
    ask_out[...] = jnp.broadcast_to(asked, (8, ASKS))
    requests = []
    for i, step in enumerate(reach):
        copy = pltpu.make_async_remote_copy(
            src_ref=ask_out,
            dst_ref=ask_in.at[i],
            send_sem=ask_send.at[i],
            recv_sem=ask_recv.at[i],
            device_id=device(step),
            device_id_type=MESH,
        )
        copy.start()
        requests.append(copy)

    predict(present, 1, 8, finish_first)

    def table_block(b, carry):
        codes = info[b, pl.ds(18, 4), :]
        kinds = lax.broadcasted_iota(jnp.int32, (16, LANES), 0).astype(F32)
        marks = [jnp.where(kinds == codes[f : f + 1], 1.0, 0.0).astype(BF16) for f in range(4)]
        marks = jnp.concatenate(marks, axis=1)
        value = dot(table_ref[...], jnp.concatenate([marks, marks], axis=0))
        for f in range(4):
            tables[4 * b + f] = value[:, LANES * f : LANES * (f + 1)]
        return carry

    lax.fori_loop(0, BLOCKS, table_block, 0)

    for copy in requests:
        copy.wait()
    asker = lax.broadcasted_iota(jnp.int32, (1, ASKS), 1) // REQ
    asked = jnp.full((1, ASKS), -1.0, F32)
    for i in range(len(reach)):
        asked = jnp.where(asker == i, ask_in[i, 0:1, :], asked)
    slots = lax.broadcasted_iota(jnp.int32, (KEEP, ASKS), 0).astype(F32)
    wanted[...] = jnp.where(slots == asked, 1.0, 0.0).astype(BF16)

    def exchange(field, turn_index):
        for b in range(KEPT_BLOCKS):
            high, low = split(field[b])
            sources[pl.ds(0, ROWS), pl.ds(LANES * b, LANES)] = high
            sources[pl.ds(192, ROWS), pl.ds(LANES * b, LANES)] = low
        answer = dot(sources[...], wanted[...])
        answer = answer[0:ROWS] + answer[192 : 192 + ROWS]
        answer = jnp.concatenate([answer, jnp.zeros((256 - ROWS, ASKS), F32)], axis=0)
        for i in range(ASKS // LANES):
            for j in range(2):
                answer_out[turn_index, pl.ds(LANES * i, LANES), pl.ds(LANES * j, LANES)] = answer[
                    LANES * j : LANES * (j + 1), LANES * i : LANES * (i + 1)
                ].T
        copies = []
        for i, step in enumerate(reach):
            part = pl.ds(REQ * i, REQ)
            copy = pltpu.make_async_remote_copy(
                src_ref=answer_out.at[turn_index, part],
                dst_ref=answer_in.at[turn_index, part],
                send_sem=answer_send.at[turn_index, i],
                recv_sem=answer_recv.at[turn_index, i],
                device_id=device(-step),
                device_id_type=MESH,
            )
            copy.start()
            copies.append(copy)
        return copies

    def local_gather(b, carry):
        owner, local, away = owners(b)
        slots = lax.broadcasted_iota(jnp.int32, (KEEP, LANES), 0).astype(F32)
        marks = [jnp.where(slots == local[f : f + 1], 1.0, 0.0).astype(BF16) for f in range(4)]
        value = dot(sources[...], jnp.concatenate(marks, axis=1))
        value = value[0:ROWS] + value[192 : 192 + ROWS]
        for f in range(4):
            gathered[4 * b + f] = value[:, LANES * f : LANES * (f + 1)]
        return carry

    def receive(turn_index, copies):
        for copy in copies:
            copy.wait()
        for i in range(ASKS // LANES):
            for j in range(2):
                block = answer_in[turn_index, pl.ds(LANES * i, LANES), pl.ds(LANES * j, LANES)].T
                if j == 1:
                    block = block[0 : ROWS - LANES]
                high, low = split(block)
                arrived[pl.ds(LANES * j, block.shape[0]), pl.ds(LANES * i, LANES)] = high
                arrived[pl.ds(192 + LANES * j, block.shape[0]), pl.ds(LANES * i, LANES)] = low

    def face_points(b, carry):
        owner, local, away = owners(b)
        value = dot_nt_placed(b)
        for f in range(4):
            gathered[4 * b + f] = jnp.where(away[f : f + 1], value, gathered[4 * b + f])
        return carry

    def dot_nt_placed(b):
        value = lax.dot_general(
            arrived[...], placed[b], (((1,), (0,)), ((), ())), preferred_element_type=F32
        )
        return value[0:ROWS] + value[192 : 192 + ROWS]

    def evaluate(i, carry):
        total = [None] * QN
        for c in range(BN):
            column = tables[i, pl.ds(NQ * c, NQ), :]
            for q in range(QN):
                row = 16 * q + c if c < 16 else TAIL + 4 * q + c - 16
                term = gathered[i, pl.ds(row, 1), :] * column
                total[q] = term if total[q] is None else total[q] + term
        for q in range(QN):
            points[i, pl.ds(NQ * q, NQ), :] = total[q]
        return carry

    def lift(field):
        def body(b, many):
            turn(field, b, many, stiff4_ref, stiff1_ref, 4, turned)
            for group in range(3):
                inside = quad_rows(field, b, many, group)
                size = 64 if group < 2 else 16
                for f in range(4):
                    parts = [points[4 * (b + i) + f, pl.ds(64 * group, size), :] for i in range(many)]
                    beyond = parts[0] if many == 1 else jnp.concatenate(parts, axis=1)
                    right = jnp.concatenate([inside, triple(beyond)], axis=0)
                    left = face4_ref[f] if group < 2 else face1_ref[f]
                    put(faces, b, many, 216 * f + 96 * group, dot(left, right))

        in_pairs(body, BLOCKS)

    low_half = lax.broadcasted_iota(jnp.int32, (8, LANES), 0) < 4

    def change_of(b):
        def load(d, q):
            value = turned[b, pl.ds(216 * d + 24 * q, 24), :]
            for f in range(4):
                value = value - info[b, pl.ds(3 * f + d, 1), :] * faces[b, pl.ds(216 * f + 24 * q, 24), :]
            return value[0:16], value[16:24]

        change = apply_jacobian(b, load)
        skew = []
        for q in range(QN):
            value = turned[b, pl.ds(648 + 24 * q, 24), :]
            for f in range(4):
                value = value - faces[b, pl.ds(216 * f + 24 * q, 24), :]
            skew.append(value)
        tails = [
            jnp.where(low_half, skew[2 * i][16:24], skew[min(2 * i + 1, 8)][16:24]) for i in range(5)
        ]
        skew = jnp.concatenate([s[0:16] for s in skew] + tails, axis=0)
        return change - info[b, pl.ds(12, 1), :] * skew

    def update(field, turn_index, finish):
        copies = exchange(field, turn_index)
        lax.fori_loop(0, BLOCKS, local_gather, 0)
        receive(turn_index, copies)
        lax.fori_loop(0, BLOCKS, face_points, 0)
        lax.fori_loop(0, 4 * BLOCKS, evaluate, 0)
        lift(field)

        def step(b, carry):
            finish(b, change_of(b))
            return carry

        lax.fori_loop(0, BLOCKS, step, 0)

    for half in range(2):
        arrived[pl.ds(192 * half + ROWS, 8), :] = jnp.zeros((8, ASKS), BF16)
        sources[pl.ds(192 * half + ROWS, 8), :] = jnp.zeros((8, KEEP), BF16)

    def finish_middle(b, change):
        base[b] = present[b] + change

    update(first, 0, finish_middle)

    def finish_second(b, members):
        quick = info[b, pl.ds(13, 1), :] < 0.5
        second[b] = jnp.where(quick, weighted(to_first, members), second[b])

    predict(base, BLOCKS, 0, finish_second)

    def finish_last(b, change):
        value = jnp.where(info[b, pl.ds(22, 1), :] > 0.5, base[b] + change, 0.0)
        at = pl.ds(pl.multiple_of(b * LANES, LANES), LANES)
        for q in range(QN):
            out_ref[q, 0:16, at] = value[16 * q : 16 * q + 16]
            out_ref[q, 16:20, at] = value[TAIL + 4 * q : TAIL + 4 * q + 4]

    update(second, 1, finish_last)


def per_device(
    count,
    element_freedom_values,
    scaled_jacobian_matrices,
    outward_face_normals,
    largest_wave_speed,
    element_cluster_index,
    element_new_slot,
    neighbours,
    face_rotation_codes,
    deriv_mats,
    stiff_mats,
    face_eval,
    face_lift,
):
    vmem = pl.BlockSpec(memory_space=pltpu.VMEM)
    consts = constants(deriv_mats, stiff_mats, face_eval, face_lift)
    return pl.pallas_call(
        functools.partial(kernel, count),
        out_shape=jax.ShapeDtypeStruct((QN, BN, PARTITION_SLOTS), F32),
        in_specs=[vmem, pl.BlockSpec(memory_space=pl.ANY)] + [vmem] * 13,
        out_specs=vmem,
        scratch_shapes=[
            pltpu.VMEM((3, QN, QN, PARTITION_SLOTS), F32),
            pltpu.VMEM((BLOCKS, 27, 5, 8, LANES), F32),
            pltpu.VMEM((BLOCKS, 24, LANES), F32),
            pltpu.VMEM((BLOCKS, ROWS, LANES), F32),
            pltpu.VMEM((BLOCKS, ROWS, LANES), F32),
            pltpu.VMEM((BLOCKS, ROWS, LANES), F32),
            pltpu.VMEM((BLOCKS, ROWS, LANES), F32),
            pltpu.VMEM((2, BLOCKS, ROWS, LANES), F32),
            pltpu.VMEM((BLOCKS, 864, LANES), F32),
            pltpu.VMEM((BLOCKS, 864, LANES), F32),
            pltpu.VMEM((4 * BLOCKS, TAIL, LANES), F32),
            pltpu.VMEM((4 * BLOCKS, ROWS, LANES), F32),
            pltpu.VMEM((4 * BLOCKS, BN * NQ, LANES), F32),
            pltpu.VMEM((384, KEEP), BF16),
            pltpu.VMEM((KEEP, ASKS), BF16),
            pltpu.VMEM((BLOCKS, ASKS, LANES), BF16),
            pltpu.VMEM((384, ASKS), BF16),
            pltpu.VMEM((SLAB, LANES), F32),
            pltpu.VMEM((2, LANES, SLAB), F32),
            pltpu.VMEM((8, ASKS), F32),
            pltpu.VMEM((9, 8, ASKS), F32),
            pltpu.VMEM((2, ASKS, 256), F32),
            pltpu.VMEM((2, ASKS, 256), F32),
            pltpu.SemaphoreType.DMA,
            pltpu.SemaphoreType.DMA((GROUPS,)),
            pltpu.SemaphoreType.DMA((GROUPS,)),
            pltpu.SemaphoreType.DMA((9,)),
            pltpu.SemaphoreType.DMA((9,)),
            pltpu.SemaphoreType.DMA((2, 9)),
            pltpu.SemaphoreType.DMA((2, 9)),
        ],
        compiler_params=pltpu.CompilerParams(
            collective_id=0, has_side_effects=True, vmem_limit_bytes=60 << 20
        ),
    )(
        element_freedom_values,
        scaled_jacobian_matrices,
        outward_face_normals,
        largest_wave_speed[None],
        element_cluster_index[None],
        element_new_slot[None],
        neighbours,
        face_rotation_codes,
        *consts,
    )


def solution(mesh):
    placed = (
        P(None, None, "dom"),
        P(None, None, None, "dom"),
        P(None, None, "dom"),
        P("dom"),
        P("dom"),
        P("dom"),
        P(None, "dom"),
        P(None, "dom"),
        P(),
        P(),
        P(),
        P(),
    )
    return jax.shard_map(
        functools.partial(per_device, mesh.shape["dom"]),
        mesh=mesh,
        in_specs=placed,
        out_specs=P(None, None, "dom"),
        check_vma=False,
    )
```

time: 584 us -> 106 us (0.18); the launches traced: 574 us -> 106 us
  local copies, waits for them, and re-layouts: 322 us -> 16 us
  other arithmetic: 122 us -> 6.36 us
  Pallas kernels: 0 us -> 82.1 us
  matrix products: 61 us -> 1.07 us
  starting transfers between devices: 47.7 us -> 0 us
  waiting for transfers between devices: 20.1 us -> 0 us
    gather x15 -> x9, local copies, waits for them, and re-layouts: 142 us -> 2.78 us  [the longest x7 2.1 us: grouped(): turned = jnp.swapaxes(mats, 1, 2)[:, DUP, :]]
    pallas_call x0 -> x1, Pallas kernels: none -> 82.1 us  [per_device(): pl.pallas_call(functools.partial(kernel, count), out_shape=jax.ShapeDtype...]
    reduce_sum x27 -> x0, other arithmetic: 67.9 us -> none  [the longest x8 39.5 us: jacobian_apply(): jnp.sum(element_jacobian_set[:, :, :, None, :] * turned[:, None, :, :, :]...]
    dot_general x33 -> x1, matrix products: 61 us -> 1.07 us  [constants(): jnp.einsum('fcn,fnb->fcb', face_eval[::3], face_lift, precision=lax.Preci...]
    mul x9 -> x7, local copies, waits for them, and re-layouts: 58.8 us -> 0.86 us  [the longest x6 0.74 us: grouped_points(): blown = turned[:, None, :, None, :] * eye[None, :, None, :, None]]
    scatter x7 -> x0, local copies, waits for them, and re-layouts: 55.2 us -> none  [the longest x1 17.6 us: per_device(): asks = jnp.zeros((length + 1,), jnp.int32).at[where_at].set(spot_local +...]
    all_to_all x5 -> x0, starting transfers between devices: 47.7 us -> none  [the longest x2 15.8 us: fetch_remote(): lax.all_to_all(picked, 'dom', split_axis=1, concat_axis=1, tiled=True)]
    select_n x9 -> x0, other arithmetic: 33.2 us -> none  [the longest x2 25.5 us: per_device(): jnp.take(face_eval, face_rotations, axis=0)]
  transfers between devices with their start and end apart: 5 -> 0, of which waited for: 2 -> 0; matrix products, arithmetic and copies ran while one was open for 41% -> 0% of each run, Pallas kernels for 0% -> 0%
where the time goes in v1:
time: 106 us
  Pallas kernels  82.1 us (77%)
  local copies, waits for them, and re-layouts  16 us (15%)
  other arithmetic  6.36 us (6%)
  matrix products  1.07 us (1%)
    pallas_call x1, Pallas kernels, per_device(): pl.pallas_call(functools.partial(kernel, count), out_shape=jax.ShapeDtype...  82.1 us
    unnamed x11, local copies, waits for them, and re-layouts  5.78 us
    concatenate x4, other arithmetic, stacked(): return jnp.concatenate([high, high, low], axis=-1)  3.01 us

profile of v1, /device:TPU:1, one launch (start us, length us, event | category | flops | bytes accessed | tf_op | source)
XLA Modules:
  0.0 105.9 jit_solution(10467066287939864354)
XLA Ops:
  0.1 0.7 pad_clamp_fusion
  0.7 0.8 multiply_bitcast_fusion.1
  1.6 0.6 gather_fusion.3
  2.3 0.8 negate_bitcast_fusion
  3.1 0.1 copy.120
  3.2 0.6 gather_fusion
  4.0 0.1 copy.121
  4.1 0.9 copy.130
  5.0 0.1 copy.125
  5.5 0.7 pad_maximum_fusion.7.pred1_ref
  6.2 1.1 %multiply_bitcast_fusion = (f32[4,20,20]{1,2,0:T(8,128)S(1)}, f32[20,20]{1,0:T(8,128)S(1)}) fusion(f32[4,16,20]{2,1,0:T(8,128)} %param.32, f32[12,20,16]{1,2,0:T(8,128)} %param.31), kind=kOutput, calls=%fused_computation.34 | convolution fusion | flops 310000 | bytes 73536 | tf_op jit(solution)/shard_map/fcn,fnb->fcb/dot_general | solution.py:76
  7.3 0.1 copy.141
  7.5 0.6 gather_fusion.1
  8.1 0.6 gather_fusion.2
  8.9 0.1 copy.156
  9.2 0.7 concatenate.81.face1_ref
  9.9 0.1 copy.131
  10.1 0.1 copy.137
  10.6 0.7 pad_maximum_fusion.5.stiff1_ref
  11.3 0.7 copy.153.normal_ref
  12.0 0.1 mul.85
  12.2 0.1 copy.151
  12.4 0.1 reshape.89
  12.5 0.7 copy.154.table_ref
  13.3 0.1 broadcast_multiply_fusion.2
  13.5 0.2 reshape.81
  13.7 0.1 reshape.82
  13.9 0.1 copy.123
  14.0 0.1 reduce-precision_convert_fusion.3
  14.1 0.8 pad_maximum_fusion.4.pred4_ref
  15.0 0.3 mul.83
  15.3 0.1 copy.150
  15.5 0.3 broadcast_multiply_fusion
  15.8 0.3 concatenate.73
  16.1 0.1 concatenate.74
  16.2 0.1 copy.144
  16.5 0.5 reshape.85
  17.0 0.1 reshape.86
  17.2 0.1 copy.134
  17.3 0.1 copy.145
  17.4 0.1 fusion.1
  17.5 1.0 concatenate.76.face4_ref
  18.6 0.1 copy.135
  18.7 0.1 reduce-precision_convert_fusion.2
  18.8 0.8 pad_maximum_fusion.1.stiff4_ref
  19.7 1.9 %copy.152.jac_hbm = f32[3,9,9,1024]{3,2,1,0:T(8,128)} copy(f32[3,9,9,1024]{3,0,2,1:T(4,128)S(1)} %copy-done) | data formatting | bytes 1990656 | tf_op args[1]
  21.5 82.1 %shard_map.199 = f32[9,20,1152]{2,1,0:T(8,128)} custom-call(f32[9,20,1024]{2,1,0:T(8,128)} %x_ref.1, f32[3,9,9,1024]{3,2,1,0:T(8,128)} %copy.152.jac_hbm, f32[4,3,1024]{2,1,0:T(4,128)} %copy.153.normal_ref, f32[1,1024]{1,0:T(1,128)} %bitcast.72, s32[1,1024]{1,0:T(1,128)} %bitcast.73, s32[1,1024]{1,0:T(1,128)} %bitcast.74, s32[4,1024]{1,0:T(4,128)} %link_ref.1, ...), custom_call_target="tpu_custom_call" | custom-call | tf_op jit(solution)/shard_map/pallas_call | solution.py:592
  103.7 2.2 %copy.163 = f32[9,20,1152]{2,1,0:T(8,128)} copy(f32[9,20,1152]{2,1,0:T(8,128)} %shard_map.199) | data formatting | bytes 1658880
  (49 shorter events, 2.5 us)
Async XLA Ops:
  0.0 11.3 %copy-start.2 = (f32[4,3,1024]{2,0,1:T(4,128)S(1)}, f32[4,3,1024]{2,0,1:T(4,128)}, u32[]{:S(2)}) copy-start(f32[4,3,1024]{2,0,1:T(4,128)} %param.23) | copy-start | bytes 147460
  3.1 9.1 %copy-start.1 = (f32[12,20,16]{1,2,0:T(8,128)S(1)}, f32[12,20,16]{1,2,0:T(8,128)}, u32[]{:S(2)}) copy-start(f32[12,20,16]{1,2,0:T(8,128)} %param.31) | copy-start | bytes 46084
  17.0 2.7 %copy-start = (f32[3,9,9,1024]{3,0,2,1:T(4,128)S(1)}, f32[3,9,9,1024]{3,0,2,1:T(4,128)}, u32[]{:S(2)}) copy-start(f32[3,9,9,1024]{3,0,2,1:T(4,128)} %param.22) | copy-start | bytes 2985988

commit v2 on v1

v2 whole, which is shorter than its diff:
```python
import functools
import math

import jax
import jax.numpy as jnp
from jax import lax
from jax.experimental import pallas as pl
from jax.experimental.pallas import tpu as pltpu
from jax.sharding import PartitionSpec as P

NORDER = 4
CSZ = 16
GROUPS = 8
E_DEV = 1024
KEEP = 896
PARTITION_SLOTS = 1152
REQ = 32
NQ = 16
QN = 9
BN = 20
LANES = 128
BLOCKS = PARTITION_SLOTS // LANES
KEPT_BLOCKS = KEEP // LANES
ROWS = 184
TAIL = 144
SLAB = 512
ASKS = 384
STEP = 0.25
F32 = jnp.float32
BF16 = jnp.bfloat16
MESH = pl.DeviceIdType.MESH


def coefficients(lower, upper):
    return [
        (upper ** (degree + 1) - lower ** (degree + 1)) / math.factorial(degree + 1)
        for degree in range(NORDER)
    ]


def dot(a, b):
    return jnp.dot(a, b, preferred_element_type=F32)


def dot_nt(a, b):
    return lax.dot_general(a, b, (((1,), (1,)), ((), ())), preferred_element_type=F32)


def split(value):
    high = value.astype(BF16)
    return high, (value - high.astype(F32)).astype(BF16)


def triple(value):
    high, low = split(value)
    return jnp.concatenate([high, low, high], axis=0)


def lanes_of(ref, first, many, start, size):
    parts = [ref[first + i, pl.ds(start, size), :] for i in range(many)]
    return parts[0] if many == 1 else jnp.concatenate(parts, axis=1)


def quad_rows(ref, first, many, group):
    if group < 2:
        main = lanes_of(ref, first, many, 64 * group, 64)
        tail = lanes_of(ref, first, many, TAIL + 16 * group, 16)
        return triple(jnp.concatenate([main, tail], axis=0))
    main = lanes_of(ref, first, many, 128, 16)
    tail = lanes_of(ref, first, many, TAIL + 32, 8)
    blank = jnp.zeros((8, main.shape[1]), F32)
    return triple(jnp.concatenate([main, tail, blank], axis=0))


def put(ref, first, many, start, value):
    for i in range(many):
        ref[first + i, pl.ds(start, value.shape[0]), :] = value[:, LANES * i : LANES * (i + 1)]


def one_hot(test):
    return jnp.where(test, 1.0, 0.0).astype(BF16)


def grid_of(rows, columns):
    shape = (rows, columns)
    return lax.broadcasted_iota(jnp.int32, shape, 0), lax.broadcasted_iota(jnp.int32, shape, 1)


def band(value, width):
    return sum(jnp.where(value >= width * i, 1, 0) for i in range(1, 4))


def f32_split(value):
    high = value.astype(BF16).astype(F32)
    return high, value - high


def build_constants(deriv_ref, stiff_ref, eval_ref, lift_ref, pred4, pred1, stiff4, stiff1, lift4, lift1, table):
    r, c = grid_of(24, BN)
    expand = one_hot((r == c) | ((r == c + 4) & (r >= BN)))

    def columns(depth, width, section, code):
        r, j = grid_of(depth, 3 * width)
        which = band(j, width)
        hit = code(j - width * which) == r
        return one_hot(hit & (which < 2)), one_hot(hit & (which == 2)), section

    four = columns(BN, 80, None, lambda j: jnp.where(j < 64, j & 15, 16 + (j & 3)))
    one = columns(BN, 32, None, lambda j: j)
    four_points = columns(NQ, 64, None, lambda j: j & 15)
    one_points = columns(NQ, 16, None, lambda j: j)

    def same(rows, height, width, owner):
        i, j = grid_of(4 * height, 3 * width)
        return band(i, height) == owner(j - width * band(j, width))

    def owner80(j):
        return jnp.where(j < 64, j >> 4, (j - 64) >> 2)

    same24 = same(96, 24, 80, owner80)
    same16 = same(64, 16, 80, owner80)
    same_points = same(96, 24, 64, lambda j: j >> 4)

    def place(high, low, selectors):
        return dot(high.astype(BF16), selectors[0]) + dot(low.astype(BF16), selectors[1])

    def both(high, low, four_to, one_to, mask, selectors4, selectors1):
        tall = [jnp.concatenate([part] * 4, axis=0) for part in (high, low)]
        four_to[...] = jnp.where(mask, place(tall[0], tall[1], selectors4), 0.0).astype(BF16)
        one_to[...] = place(high, low, selectors1).astype(BF16)

    def rows_of(matrix):
        high, low = f32_split(matrix)
        return dot_nt(expand, high.astype(BF16)), dot_nt(expand, low.astype(BF16))

    for d in range(3):
        high, low = rows_of(-deriv_ref[d])
        both(high, low, pred4.at[pl.ds(96 * d, 96)], pred1.at[d], same24, four, one)
        high, low = rows_of(stiff_ref[d])
        both(high, low, stiff4.at[pl.ds(96 * d, 96)], stiff1.at[pl.ds(24 * d, 24)], same24, four, one)
    own = None
    for f in range(4):
        high, low = rows_of(lift_ref[f])
        values = eval_ref[3 * f]
        term = jnp.dot(high + low, values, precision=lax.Precision.HIGHEST, preferred_element_type=F32)
        own = term if own is None else own + term
        both(0.5 * high, 0.5 * low, lift4.at[f], lift1.at[f], same_points, four_points, one_points)
        high, low = f32_split(values)
        both(high, low, stiff4.at[pl.ds(384 + 64 * f, 64)], stiff1.at[pl.ds(96 + 16 * f, 16)], same16, four, one)
    high, low = f32_split(own)
    both(high, low, stiff4.at[pl.ds(288, 96)], stiff1.at[pl.ds(72, 24)], same24, four, one)

    r, j = grid_of(BN * NQ, BN)
    pick = one_hot((r >> 4) == j)
    r, j = grid_of(BN * NQ, 12 * NQ)
    level = (r & 15) == (j & 15)
    r, j = grid_of(12 * NQ, 32)
    kind_high, kind_low = one_hot((r >> 4) == j), one_hot((r >> 4) + 16 == j)
    high, low = f32_split(eval_ref[...].reshape(12 * NQ, BN))
    high = jnp.where(level, dot_nt(pick, high.astype(BF16)), 0.0)
    low = jnp.where(level, dot_nt(pick, low.astype(BF16)), 0.0)
    table[...] = (dot(high.astype(BF16), kind_high) + dot(low.astype(BF16), kind_low)).astype(BF16)


def kernel(
    count,
    x_ref,
    jac_hbm,
    normal_ref,
    speed_ref,
    cluster_ref,
    slot_ref,
    link_ref,
    turn_ref,
    deriv_ref,
    stiff_ref,
    eval_ref,
    lift_ref,
    out_ref,
    pred4,
    pred1,
    stiff4,
    stiff1,
    lift4,
    lift1,
    table,
    jac,
    pairs,
    info,
    present,
    first,
    second,
    base,
    series,
    turned,
    faces,
    points,
    gathered,
    tables,
    sources,
    marks,
    wanted,
    placed,
    arrived,
    pack,
    got,
    ask_out,
    ask_in,
    answer_out,
    answer_in,
    jac_sem,
    pack_send,
    pack_recv,
    ask_send,
    ask_recv,
    answer_send,
    answer_recv,
):
    me = lax.axis_index("dom")
    group_steps = [max(g * (count // GROUPS), 1) for g in range(GROUPS)]
    reach = [1, 2, 3, 4, count - 1, count - 2, count - 3, count - 4, count // 2]
    greeted = sorted(
        {s % count for s in group_steps} | {-s % count for s in group_steps} | {s % count for s in reach}
    )

    def device(step):
        return (lax.rem(me + (step % count), count),)

    barrier = pltpu.get_barrier_semaphore()
    for step in greeted:
        pl.semaphore_signal(barrier, inc=1, device_id=device(step), device_id_type=MESH)

    jac_copy = pltpu.make_async_copy(jac_hbm, jac.at[:, :, :, pl.ds(0, E_DEV)], jac_sem)
    jac_copy.start()

    answer_in[:, pl.ds(288, 96), :] = jnp.zeros((2, 96, 256), F32)
    for half in range(2):
        arrived[pl.ds(192 * half + ROWS, 8), :] = jnp.zeros((8, ASKS), BF16)
        sources[pl.ds(192 * half + ROWS, 8), :] = jnp.zeros((8, KEEP), BF16)

    def load_block(b, carry):
        at = pl.ds(pl.multiple_of(b * LANES, LANES), LANES)
        for q in range(QN):
            present[b, pl.ds(16 * q, 16), :] = x_ref[q, 0:16, at]
            present[b, pl.ds(TAIL + 4 * q, 4), :] = x_ref[q, 16:20, at]
        present[b, pl.ds(180, 4), :] = jnp.zeros((4, LANES), F32)
        for d in range(3):
            info[b, pl.ds(4 * d, 4), :] = normal_ref[d, :, at]
        info[b, pl.ds(12, 1), :] = speed_ref[:, at]
        info[b, pl.ds(13, 1), :] = cluster_ref[:, at].astype(F32)
        info[b, pl.ds(14, 4), :] = link_ref[:, at].astype(F32)
        info[b, pl.ds(18, 4), :] = turn_ref[:, at].astype(F32)
        info[b, pl.ds(22, 2), :] = jnp.ones((2, LANES), F32)
        return carry

    lax.fori_loop(0, 8, load_block, 0)
    lane = lax.broadcasted_iota(jnp.int32, (1, LANES), 1)
    leaves = slot_ref[:, KEEP:E_DEV] != me * PARTITION_SLOTS + KEEP + lane

    pack[pl.ds(0, ROWS), :] = jnp.where(leaves, present[7], 0.0)
    pack[pl.ds(ROWS, 24), :] = jnp.where(leaves, info[7], 0.0)
    pack[pl.ds(451, SLAB - 451), :] = jnp.zeros((SLAB - 451, LANES), F32)
    info[7, pl.ds(22, 1), :] = jnp.where(leaves, 0.0, 1.0)
    jac_copy.wait()
    for p in range(QN):
        for q in range(QN):
            pack[pl.ds(208 + 3 * (9 * p + q), 3), :] = jnp.where(
                leaves, jac[p, q, :, pl.ds(KEEP, LANES)], 0.0
            )
    for i in range(SLAB // LANES):
        got[0, :, pl.ds(LANES * i, LANES)] = pack[pl.ds(LANES * i, LANES), :].T

    pl.semaphore_wait(barrier, len(greeted))

    moves = []
    for g, step in enumerate(group_steps):
        part = pl.ds(CSZ * g, CSZ)
        copy = pltpu.make_async_remote_copy(
            src_ref=got.at[0, part],
            dst_ref=got.at[1, part],
            send_sem=pack_send.at[g],
            recv_sem=pack_recv.at[g],
            device_id=device(step),
            device_id_type=MESH,
        )
        copy.start()
        moves.append(copy)

    low_half = lax.broadcasted_iota(jnp.int32, (8, LANES), 0) < 4

    def pair_block(b, carry):
        at = pl.ds(pl.multiple_of(b * LANES, LANES), LANES)
        for d in range(3):
            for q in range(QN):
                for i in range(5):
                    upper = jac[min(2 * i + 1, 8), q, d : d + 1, at]
                    pairs[b, 9 * d + q, i] = jnp.where(low_half, jac[2 * i, q, d : d + 1, at], upper)
        return carry

    def turn(ref, first_block, many):
        for group in range(3):
            right = quad_rows(ref, first_block, many, group)
            if group < 2:
                result = dot(pred4[...], right)
                for d in range(3):
                    put(turned, first_block, many, 216 * d + 96 * group, result[96 * d : 96 * (d + 1)])
            else:
                result = dot(pred1[...].reshape(72, 96), right)
                for d in range(3):
                    put(turned, first_block, many, 216 * d + 192, result[24 * d : 24 * (d + 1)])

    def apply_jacobian(b, load_turned):
        at = pl.ds(pl.multiple_of(b * LANES, LANES), LANES)
        main = None
        tail = None
        for d in range(3):
            for q in range(QN):
                upper, lower = load_turned(d, q)
                column = jac[:, q, d : d + 1, at]
                one = column * upper[None]
                two = pairs[b, 9 * d + q] * lower[None]
                main = one if main is None else main + one
                tail = two if tail is None else tail + two
        return jnp.concatenate([main.reshape(TAIL, LANES), tail.reshape(40, LANES)], axis=0)

    def plain_turned(b):
        def load(d, q):
            value = turned[b, pl.ds(216 * d + 24 * q, 24), :]
            return value[0:16], value[16:24]

        return load

    to_first = coefficients(0.0, STEP)
    to_slow = coefficients(STEP, 2.0 * STEP)

    def pipelined(prepare, use, start, blocks):
        whole = blocks // 2

        def step(i, carry):
            use(start + 2 * i, 2)
            prepare(start + 2 * i + 2, 2)
            return carry

        lax.fori_loop(0, whole - 1, step, 0)
        if blocks % 2:
            use(start + 2 * whole - 2, 2)
            prepare(start + 2 * whole, 1)
            return lambda: use(start + 2 * whole, 1)
        return lambda: use(start + 2 * whole - 2, 2)

    def predict(field, start, blocks, finish):
        def source(degree):
            return field if degree == 0 else series.at[degree - 1]

        turn(source(0), start, 2)
        for degree in range(NORDER - 1):

            def use(b, many, degree=degree):
                for i in range(many):
                    value = apply_jacobian(b + i, plain_turned(b + i))
                    if degree < NORDER - 2:
                        series[degree, b + i] = value
                    else:
                        finish(b + i, [field[b + i], series[0, b + i], series[1, b + i], value])

            def prepare(b, many, degree=degree):
                turn(source(degree), b, many)

            last = pipelined(prepare, use, start, blocks)
            if degree < NORDER - 2 and blocks > 2:
                last()
                turn(source(degree + 1), start, 2)
            else:
                last()
                if degree < NORDER - 2:
                    turn(source(degree + 1), start, 2)

    def weighted(factors, members):
        total = factors[0] * members[0]
        for factor, member in zip(factors[1:], members[1:]):
            total = total + factor * member
        return total

    def finish_first(b, members):
        first[b] = weighted(to_first, members)
        second[b] = weighted(to_slow, members)

    build_constants(
        deriv_ref, stiff_ref, eval_ref, lift_ref, pred4, pred1, stiff4, stiff1, lift4, lift1, table
    )
    lax.fori_loop(0, 8, pair_block, 0)

    for copy in moves:
        copy.wait()
    for i in range(SLAB // LANES):
        pack[pl.ds(LANES * i, LANES), :] = got[1, :, pl.ds(LANES * i, LANES)].T
    present[8] = pack[pl.ds(0, ROWS), :]
    info[8] = pack[pl.ds(ROWS, 24), :]
    for p in range(QN):
        for q in range(QN):
            jac[p, q, :, pl.ds(E_DEV, LANES)] = pack[pl.ds(208 + 3 * (9 * p + q), 3), :]
    pair_block(8, 0)

    which = lax.broadcasted_iota(jnp.int32, (16, LANES), 0)
    near = jnp.where(which < 4, which + 1, count + 3 - which)
    wanted_step = jnp.where(which < 8, near, jnp.where(which == 8, count // 2, -7)).astype(F32)
    row_f = which.astype(F32)
    me_f = (jnp.zeros((1, LANES), jnp.int32) + me).astype(F32)
    r, c = grid_of(LANES, 2 * LANES)
    sums = one_hot(r < c)

    def owners(b):
        link = info[b, pl.ds(14, 4), :]
        owner = jnp.floor((link + 0.5) * (1.0 / PARTITION_SLOTS))
        local = link - owner * PARTITION_SLOTS
        away = jnp.where(owner != me_f, info[b, pl.ds(22, 1), :], 0.0) > 0.5
        return owner, local, away

    def scan(b, carry):
        running, asked = carry
        owner, local, away = owners(b)
        step = owner - me_f
        step = jnp.where(step < 0.0, step + count, step)
        step = jnp.max(jnp.where(away, step, -1.0), axis=0, keepdims=True)
        spot = jnp.max(jnp.where(away, local, 0.0), axis=0, keepdims=True)
        hit = wanted_step == step
        member = jnp.where(hit, 1.0, 0.0)
        prefix = dot(member.astype(BF16), sums)
        place = jnp.where(hit, 32.0 * row_f + running + prefix[:, :LANES], 0.0)
        found = jnp.sum(member, axis=0, keepdims=True)
        place = jnp.sum(place, axis=0, keepdims=True) - (1.0 - found)
        high = jnp.floor(spot * 0.125)
        text = jnp.concatenate([high, spot - 8.0 * high, found, jnp.zeros((13, LANES), F32)], axis=0)
        rows = lax.broadcasted_iota(jnp.int32, (ASKS, LANES), 0).astype(F32)
        chosen = one_hot(rows == place)
        placed[b] = chosen
        asked = asked + dot_nt(text.astype(BF16), chosen)
        return running + prefix[:, LANES:], asked

    _, asked = lax.fori_loop(
        0, BLOCKS, scan, (jnp.zeros((16, LANES), F32), jnp.zeros((16, ASKS), F32))
    )
    asked = jnp.where(asked[2:3] > 0.5, 8.0 * asked[0:1] + asked[1:2], -1.0)
    ask_out[...] = jnp.broadcast_to(asked, (8, ASKS))
    requests = []
    for i, step in enumerate(reach):
        copy = pltpu.make_async_remote_copy(
            src_ref=ask_out,
            dst_ref=ask_in.at[i],
            send_sem=ask_send.at[i],
            recv_sem=ask_recv.at[i],
            device_id=device(step),
            device_id_type=MESH,
        )
        copy.start()
        requests.append(copy)

    predict(present, 0, BLOCKS, finish_first)

    for copy in requests:
        copy.wait()
    asker = lax.broadcasted_iota(jnp.int32, (1, ASKS), 1) // REQ
    asked = jnp.full((1, ASKS), -1.0, F32)
    for i in range(len(reach)):
        asked = jnp.where(asker == i, ask_in[i, 0:1, :], asked)
    slots = lax.broadcasted_iota(jnp.int32, (KEEP, ASKS), 0).astype(F32)
    wanted[...] = one_hot(slots == asked)

    def exchange(field, turn_index):
        for b in range(KEPT_BLOCKS):
            high, low = split(field[b])
            sources[pl.ds(0, ROWS), pl.ds(LANES * b, LANES)] = high
            sources[pl.ds(192, ROWS), pl.ds(LANES * b, LANES)] = low
        answer = dot(sources[...], wanted[...])
        answer = answer[0:ROWS] + answer[192 : 192 + ROWS]
        answer = jnp.concatenate([answer, jnp.zeros((256 - ROWS, ASKS), F32)], axis=0)
        for i in range(ASKS // LANES):
            for j in range(2):
                answer_out[turn_index, pl.ds(LANES * i, LANES), pl.ds(LANES * j, LANES)] = answer[
                    LANES * j : LANES * (j + 1), LANES * i : LANES * (i + 1)
                ].T
        copies = []
        for i, step in enumerate(reach):
            part = pl.ds(REQ * i, REQ)
            copy = pltpu.make_async_remote_copy(
                src_ref=answer_out.at[turn_index, part],
                dst_ref=answer_in.at[turn_index, part],
                send_sem=answer_send.at[turn_index, i],
                recv_sem=answer_recv.at[turn_index, i],
                device_id=device(-step),
                device_id_type=MESH,
            )
            copy.start()
            copies.append(copy)
        return copies

    def table_block(b, carry):
        codes = info[b, pl.ds(18, 4), :]
        kinds = lax.broadcasted_iota(jnp.int32, (16, LANES), 0).astype(F32)
        chosen = jnp.concatenate([one_hot(kinds == codes[f : f + 1]) for f in range(4)], axis=1)
        value = dot(table[...], jnp.concatenate([chosen, chosen], axis=0))
        for f in range(4):
            tables[4 * b + f] = value[:, LANES * f : LANES * (f + 1)]
        return carry

    def mark_block(b, carry):
        _, local, _ = owners(b)
        slots = lax.broadcasted_iota(jnp.int32, (KEEP, LANES), 0).astype(F32)
        for f in range(4):
            marks[b, :, pl.ds(LANES * f, LANES)] = one_hot(slots == local[f : f + 1])
        return carry

    def receive(turn_index, copies):
        for copy in copies:
            copy.wait()
        for i in range(ASKS // LANES):
            for j in range(2):
                block = answer_in[turn_index, pl.ds(LANES * i, LANES), pl.ds(LANES * j, LANES)].T
                if j == 1:
                    block = block[0 : ROWS - LANES]
                high, low = split(block)
                arrived[pl.ds(LANES * j, block.shape[0]), pl.ds(LANES * i, LANES)] = high
                arrived[pl.ds(192 + LANES * j, block.shape[0]), pl.ds(LANES * i, LANES)] = low

    def gather(b):
        _, _, away = owners(b)
        value = dot(sources[...], marks[b])
        value = value[0:ROWS] + value[192 : 192 + ROWS]
        other = dot(arrived[...], placed[b])
        other = other[0:ROWS] + other[192 : 192 + ROWS]
        for f in range(4):
            gathered[4 * b + f] = jnp.where(
                away[f : f + 1], other, value[:, LANES * f : LANES * (f + 1)]
            )

    def evaluate(i):
        total = [points[i, pl.ds(NQ * q, NQ), :] for q in range(QN)]
        for c in range(BN):
            column = tables[i, pl.ds(NQ * c, NQ), :]
            for q in range(QN):
                row = 16 * q + c if c < 16 else TAIL + 4 * q + c - 16
                total[q] = total[q] + gathered[i, pl.ds(row, 1), :] * column
        for q in range(QN):
            points[i, pl.ds(NQ * q, NQ), :] = total[q]

    def inside(field, b, many):
        for group in range(3):
            right = quad_rows(field, b, many, group)
            tall = 96 if group < 2 else 24
            wide = 64 if group < 2 else 16
            result = dot(stiff4[...] if group < 2 else stiff1[...], right)
            for d in range(4):
                put(turned, b, many, 216 * d + 96 * group, result[tall * d : tall * (d + 1)])
            for f in range(4):
                part = result[4 * tall + wide * f : 4 * tall + wide * (f + 1)]
                for i in range(many):
                    points[4 * (b + i) + f, pl.ds(64 * group, wide), :] = part[
                        :, LANES * i : LANES * (i + 1)
                    ]

    def lift(b, many):
        for group in range(3):
            wide = 64 if group < 2 else 16
            for f in range(4):
                parts = [points[4 * (b + i) + f, pl.ds(64 * group, wide), :] for i in range(many)]
                right = parts[0] if many == 1 else jnp.concatenate(parts, axis=1)
                left = lift4[f] if group < 2 else lift1[f]
                put(faces, b, many, 216 * f + 96 * group, dot(left, triple(right)))

    def change_of(b):
        def load(d, q):
            value = turned[b, pl.ds(216 * d + 24 * q, 24), :]
            for f in range(4):
                value = value - info[b, pl.ds(4 * d + f, 1), :] * faces[b, pl.ds(216 * f + 24 * q, 24), :]
            return value[0:16], value[16:24]

        change = apply_jacobian(b, load)
        skew = []
        for q in range(QN):
            value = turned[b, pl.ds(648 + 24 * q, 24), :]
            for f in range(4):
                value = value - faces[b, pl.ds(216 * f + 24 * q, 24), :]
            skew.append(value)
        tails = [
            jnp.where(low_half, skew[2 * i][16:24], skew[min(2 * i + 1, 8)][16:24]) for i in range(5)
        ]
        skew = jnp.concatenate([s[0:16] for s in skew] + tails, axis=0)
        return change - info[b, pl.ds(12, 1), :] * skew

    def prepare_inside(field):
        def step(i, carry):
            inside(field, 2 * i, 2)
            return carry

        lax.fori_loop(0, BLOCKS // 2, step, 0)
        inside(field, BLOCKS - 1, 1)

    def update(turn_index, copies, finish):
        receive(turn_index, copies)
        gather(0)

        def step(b, carry):
            for f in range(4):
                evaluate(4 * b + f)
            gather(b + 1)
            return carry

        lax.fori_loop(0, BLOCKS - 1, step, 0)
        for f in range(4):
            evaluate(4 * (BLOCKS - 1) + f)
        lift(0, 2)

        def use(b, many):
            for i in range(many):
                finish(b + i, change_of(b + i))

        pipelined(lift, use, 0, BLOCKS)()

    copies = exchange(first, 0)
    lax.fori_loop(0, BLOCKS, table_block, 0)
    lax.fori_loop(0, BLOCKS, mark_block, 0)
    prepare_inside(first)

    def finish_middle(b, change):
        base[b] = present[b] + change

    update(0, copies, finish_middle)

    def finish_second(b, members):
        quick = info[b, pl.ds(13, 1), :] < 0.5
        second[b] = jnp.where(quick, weighted(to_first, members), second[b])

    predict(base, 0, KEPT_BLOCKS, finish_second)
    copies = exchange(second, 1)
    predict(base, KEPT_BLOCKS, 2, finish_second)
    prepare_inside(second)

    def finish_last(b, change):
        value = jnp.where(info[b, pl.ds(22, 1), :] > 0.5, base[b] + change, 0.0)
        at = pl.ds(pl.multiple_of(b * LANES, LANES), LANES)
        for q in range(QN):
            out_ref[q, 0:16, at] = value[16 * q : 16 * q + 16]
            out_ref[q, 16:20, at] = value[TAIL + 4 * q : TAIL + 4 * q + 4]

    update(1, copies, finish_last)


def per_device(
    count,
    element_freedom_values,
    scaled_jacobian_matrices,
    outward_face_normals,
    largest_wave_speed,
    element_cluster_index,
    element_new_slot,
    neighbours,
    face_rotation_codes,
    deriv_mats,
    stiff_mats,
    face_eval,
    face_lift,
):
    vmem = pl.BlockSpec(memory_space=pltpu.VMEM)
    return pl.pallas_call(
        functools.partial(kernel, count),
        out_shape=jax.ShapeDtypeStruct((QN, BN, PARTITION_SLOTS), F32),
        in_specs=[vmem, pl.BlockSpec(memory_space=pl.ANY)] + [vmem] * 10,
        out_specs=vmem,
        scratch_shapes=[
            pltpu.VMEM((288, 240), BF16),
            pltpu.VMEM((3, 24, 96), BF16),
            pltpu.VMEM((640, 240), BF16),
            pltpu.VMEM((160, 96), BF16),
            pltpu.VMEM((4, 96, 192), BF16),
            pltpu.VMEM((4, 24, 48), BF16),
            pltpu.VMEM((BN * NQ, 32), BF16),
            pltpu.VMEM((QN, QN, 3, PARTITION_SLOTS), F32),
            pltpu.VMEM((BLOCKS, 27, 5, 8, LANES), F32),
            pltpu.VMEM((BLOCKS, 24, LANES), F32),
            pltpu.VMEM((BLOCKS, ROWS, LANES), F32),
            pltpu.VMEM((BLOCKS, ROWS, LANES), F32),
            pltpu.VMEM((BLOCKS, ROWS, LANES), F32),
            pltpu.VMEM((BLOCKS, ROWS, LANES), F32),
            pltpu.VMEM((2, BLOCKS, ROWS, LANES), F32),
            pltpu.VMEM((BLOCKS, 864, LANES), F32),
            pltpu.VMEM((BLOCKS, 864, LANES), F32),
            pltpu.VMEM((4 * BLOCKS, TAIL, LANES), F32),
            pltpu.VMEM((4 * BLOCKS, ROWS, LANES), F32),
            pltpu.VMEM((4 * BLOCKS, BN * NQ, LANES), F32),
            pltpu.VMEM((384, KEEP), BF16),
            pltpu.VMEM((BLOCKS, KEEP, 4 * LANES), BF16),
            pltpu.VMEM((KEEP, ASKS), BF16),
            pltpu.VMEM((BLOCKS, ASKS, LANES), BF16),
            pltpu.VMEM((384, ASKS), BF16),
            pltpu.VMEM((SLAB, LANES), F32),
            pltpu.VMEM((2, LANES, SLAB), F32),
            pltpu.VMEM((8, ASKS), F32),
            pltpu.VMEM((9, 8, ASKS), F32),
            pltpu.VMEM((2, ASKS, 256), F32),
            pltpu.VMEM((2, ASKS, 256), F32),
            pltpu.SemaphoreType.DMA,
            pltpu.SemaphoreType.DMA((GROUPS,)),
            pltpu.SemaphoreType.DMA((GROUPS,)),
            pltpu.SemaphoreType.DMA((9,)),
            pltpu.SemaphoreType.DMA((9,)),
            pltpu.SemaphoreType.DMA((2, 9)),
            pltpu.SemaphoreType.DMA((2, 9)),
        ],
        compiler_params=pltpu.CompilerParams(
            collective_id=0, has_side_effects=True, vmem_limit_bytes=60 << 20
        ),
    )(
        element_freedom_values,
        jnp.transpose(scaled_jacobian_matrices, (1, 2, 0, 3)),
        jnp.transpose(outward_face_normals, (1, 0, 2)),
        largest_wave_speed[None],
        element_cluster_index[None],
        element_new_slot[None],
        neighbours,
        face_rotation_codes,
        deriv_mats,
        stiff_mats,
        jnp.swapaxes(face_eval, 1, 2),
        face_lift,
    )


def solution(mesh):
    placed = (
        P(None, None, "dom"),
        P(None, None, None, "dom"),
        P(None, None, "dom"),
        P("dom"),
        P("dom"),
        P("dom"),
        P(None, "dom"),
        P(None, "dom"),
        P(),
        P(),
        P(),
        P(),
    )
    return jax.shard_map(
        functools.partial(per_device, mesh.shape["dom"]),
        mesh=mesh,
        in_specs=placed,
        out_specs=P(None, None, "dom"),
        check_vma=False,
    )
```

time: 106 us -> 79.4 us (0.75)
  local copies, waits for them, and re-layouts: 16 us -> 2.22 us
  other arithmetic: 6.36 us -> 0 us
  Pallas kernels: 82.1 us -> 77 us
  matrix products: 1.07 us -> 0 us
    pallas_call x1, Pallas kernels: 82.1 us -> 77 us  [per_device(): pl.pallas_call(functools.partial(kernel, count), out_shape=jax.ShapeDtype...]
    unnamed x11 -> x1, local copies, waits for them, and re-layouts: 5.78 us -> 2.22 us
    concatenate x12 -> x0, local copies, waits for them, and re-layouts: 3.43 us -> none  [the longest x2 1.77 us: constants(): result.append(jnp.concatenate([inside, beyond], axis=-1))]
    concatenate x5 -> x0, other arithmetic: 3.01 us -> none  [the longest x4 3.01 us: stacked(): return jnp.concatenate([high, high, low], axis=-1)]
    gather x9 -> x0, local copies, waits for them, and re-layouts: 2.78 us -> none  [the longest x7 2.1 us: grouped(): turned = jnp.swapaxes(mats, 1, 2)[:, DUP, :]]
    reshape x13 -> x0, local copies, waits for them, and re-layouts: 1.83 us -> none  [the longest x6 1.08 us: grouped(): main = blown[..., :16].reshape(rows, many * 16)]
    transpose x3 -> x0, other arithmetic: 1.56 us -> none  [the longest x2 0.8 us: grouped(): turned = jnp.swapaxes(mats, 1, 2)[:, DUP, :]]
    dot_general x1 -> x0, matrix products: 1.07 us -> none  [constants(): jnp.einsum('fcn,fnb->fcb', face_eval[::3], face_lift, precision=lax.Preci...]
where the time goes in v2:
time: 79.4 us; the launch traced here: 79.2 us
  Pallas kernels  77 us (97%)
  local copies, waits for them, and re-layouts  2.22 us (3%)
    pallas_call x1, Pallas kernels, per_device(): pl.pallas_call(functools.partial(kernel, count), out_shape=jax.ShapeDtype...  77 us
    unnamed x1, local copies, waits for them, and re-layouts  2.22 us

profile of v2, /device:TPU:1, one launch (start us, length us, event | category | flops | bytes accessed | tf_op | source)
XLA Modules:
  0.0 79.2 jit_solution(2347984717521353939)
XLA Ops:
  0.0 77.0 %shard_map.118 = f32[9,20,1152]{2,1,0:T(8,128)} custom-call(f32[9,20,1024]{2,1,0:T(8,128)} %x_ref.1, f32[9,9,3,1024]{3,2,1,0:T(4,128)} %bitcast.6, f32[3,4,1024]{2,1,0:T(4,128)} %bitcast.8, f32[1,1024]{1,0:T(1,128)} %bitcast.9, s32[1,1024]{1,0:T(1,128)} %bitcast.10, s32[1,1024]{1,0:T(1,128)} %bitcast.11, s32[4,1024]{1,0:T(4,128)} %link_ref.1, ...), custom_call_target="tpu_custom_call" | custom-call | tf_op jit(solution)/shard_map/pallas_call | solution.py:664
  77.0 2.2 %copy.14 = f32[9,20,1152]{2,1,0:T(8,128)} copy(f32[9,20,1152]{2,1,0:T(8,128)} %shard_map.118) | data formatting | bytes 1658880

commit v3 on v2

--- a/solution.py
+++ b/solution.py
@@ -56,25 +56,36 @@
     return jnp.concatenate([high, low, high], axis=0)
 
 
-def lanes_of(ref, first, many, start, size):
-    parts = [ref[first + i, pl.ds(start, size), :] for i in range(many)]
-    return parts[0] if many == 1 else jnp.concatenate(parts, axis=1)
-
-
-def quad_rows(ref, first, many, group):
+def lanes_of(ref, first, start, size):
+    return jnp.concatenate([ref[first + i, pl.ds(start, size), :] for i in range(2)], axis=1)
+
+
+def quad_rows(ref, first, group):
     if group < 2:
-        main = lanes_of(ref, first, many, 64 * group, 64)
-        tail = lanes_of(ref, first, many, TAIL + 16 * group, 16)
+        main = lanes_of(ref, first, 64 * group, 64)
+        tail = lanes_of(ref, first, TAIL + 16 * group, 16)
         return triple(jnp.concatenate([main, tail], axis=0))
-    main = lanes_of(ref, first, many, 128, 16)
-    tail = lanes_of(ref, first, many, TAIL + 32, 8)
+    main = lanes_of(ref, first, 128, 16)
+    tail = lanes_of(ref, first, TAIL + 32, 8)
     blank = jnp.zeros((8, main.shape[1]), F32)
     return triple(jnp.concatenate([main, tail, blank], axis=0))
 
 
-def put(ref, first, many, start, value):
-    for i in range(many):
+def put(ref, first, start, value):
+    for i in range(2):
         ref[first + i, pl.ds(start, value.shape[0]), :] = value[:, LANES * i : LANES * (i + 1)]
+
+
+def run(steps):
+    for _ in steps:
+        pass
+
+
+def together(main, side, every):
+    for count, _ in enumerate(main):
+        if count % every == 0:
+            next(side, None)
+    run(side)
 
 
 def one_hot(test):
@@ -191,11 +202,16 @@
     first,
     second,
     base,
-    series,
-    turned,
-    faces,
+    series0,
+    series1,
+    turned0,
+    turned1,
+    volume,
+    faces0,
+    faces1,
     points,
-    gathered,
+    gathered0,
+    gathered1,
     tables,
     sources,
     marks,
@@ -234,6 +250,9 @@
     jac_copy.start()
 
     answer_in[:, pl.ds(288, 96), :] = jnp.zeros((2, 96, 256), F32)
+    for field in (present, first, second, base, series0, series1):
+        field[BLOCKS] = jnp.zeros((ROWS, LANES), F32)
+    info[BLOCKS] = jnp.zeros((24, LANES), F32)
     for half in range(2):
         arrived[pl.ds(192 * half + ROWS, 8), :] = jnp.zeros((8, ASKS), BF16)
         sources[pl.ds(192 * half + ROWS, 8), :] = jnp.zeros((8, KEEP), BF16)
@@ -270,6 +289,22 @@
     for i in range(SLAB // LANES):
         got[0, :, pl.ds(LANES * i, LANES)] = pack[pl.ds(LANES * i, LANES), :].T
 
+    low_half = lax.broadcasted_iota(jnp.int32, (8, LANES), 0) < 4
+
+    def pair_block(b, carry):
+        at = pl.ds(pl.multiple_of(b * LANES, LANES), LANES)
+        for d in range(3):
+            for q in range(QN):
+                for i in range(5):
+                    upper = jac[min(2 * i + 1, 8), q, d : d + 1, at]
+                    pairs[b, 9 * d + q, i] = jnp.where(low_half, jac[2 * i, q, d : d + 1, at], upper)
+        return carry
+
+    build_constants(
+        deriv_ref, stiff_ref, eval_ref, lift_ref, pred4, pred1, stiff4, stiff1, lift4, lift1, table
+    )
+    lax.fori_loop(0, 8, pair_block, 0)
+
     pl.semaphore_wait(barrier, len(greeted))
 
     moves = []
@@ -286,28 +321,16 @@
         copy.start()
         moves.append(copy)
 
-    low_half = lax.broadcasted_iota(jnp.int32, (8, LANES), 0) < 4
-
-    def pair_block(b, carry):
-        at = pl.ds(pl.multiple_of(b * LANES, LANES), LANES)
-        for d in range(3):
-            for q in range(QN):
-                for i in range(5):
-                    upper = jac[min(2 * i + 1, 8), q, d : d + 1, at]
-                    pairs[b, 9 * d + q, i] = jnp.where(low_half, jac[2 * i, q, d : d + 1, at], upper)
-        return carry
-
-    def turn(ref, first_block, many):
+    def turn(ref, b, target):
         for group in range(3):
-            right = quad_rows(ref, first_block, many, group)
-            if group < 2:
-                result = dot(pred4[...], right)
-                for d in range(3):
-                    put(turned, first_block, many, 216 * d + 96 * group, result[96 * d : 96 * (d + 1)])
-            else:
-                result = dot(pred1[...].reshape(72, 96), right)
-                for d in range(3):
-                    put(turned, first_block, many, 216 * d + 192, result[24 * d : 24 * (d + 1)])
+            right = quad_rows(ref, b, group)
+            yield
+            tall = 96 if group < 2 else 24
+            result = dot(pred4[...] if group < 2 else pred1[...].reshape(72, 96), right)
+            yield
+            for d in range(3):
+                put(target, 0, 216 * d + 96 * group, result[tall * d : tall * (d + 1)])
+                yield
 
     def apply_jacobian(b, load_turned):
         at = pl.ds(pl.multiple_of(b * LANES, LANES), LANES)
@@ -321,59 +344,64 @@
                 two = pairs[b, 9 * d + q] * lower[None]
                 main = one if main is None else main + one
                 tail = two if tail is None else tail + two
+                yield
         return jnp.concatenate([main.reshape(TAIL, LANES), tail.reshape(40, LANES)], axis=0)
-
-    def plain_turned(b):
-        def load(d, q):
-            value = turned[b, pl.ds(216 * d + 24 * q, 24), :]
-            return value[0:16], value[16:24]
-
-        return load
 
     to_first = coefficients(0.0, STEP)
     to_slow = coefficients(STEP, 2.0 * STEP)
 
-    def pipelined(prepare, use, start, blocks):
-        whole = blocks // 2
+    def alternate(prepare, use, start, blocks, buffers, then, every):
+        whole = (blocks + 1) // 2
+        here, there = buffers
+        double = (whole - 1) // 2
 
         def step(i, carry):
-            use(start + 2 * i, 2)
-            prepare(start + 2 * i + 2, 2)
+            b = start + 4 * i
+            together(use(b, 2, here), prepare(b + 2, there), every)
+            together(use(b + 2, 2, there), prepare(b + 4, here), every)
             return carry
 
-        lax.fori_loop(0, whole - 1, step, 0)
-        if blocks % 2:
-            use(start + 2 * whole - 2, 2)
-            prepare(start + 2 * whole, 1)
-            return lambda: use(start + 2 * whole, 1)
-        return lambda: use(start + 2 * whole - 2, 2)
+        if double:
+            lax.fori_loop(0, double, step, 0)
+        if whole % 2 == 0:
+            b = start + 4 * double
+            together(use(b, 2, here), prepare(b + 2, there), every)
+            here, there = there, here
+        final = use(start + 2 * (whole - 1), 2 - blocks % 2, here)
+        if whole == 1:
+            run(final)
+            run(then(there))
+        else:
+            together(final, then(there), every)
+        return there, here
 
     def predict(field, start, blocks, finish):
-        def source(degree):
-            return field if degree == 0 else series.at[degree - 1]
-
-        turn(source(0), start, 2)
+        sources_of = [field, series0, series1]
+        buffers = (turned0, turned1)
+        run(turn(field, start, buffers[0]))
         for degree in range(NORDER - 1):
 
-            def use(b, many, degree=degree):
+            def use(b, many, buffer, degree=degree):
                 for i in range(many):
-                    value = apply_jacobian(b + i, plain_turned(b + i))
+
+                    def load(d, q, i=i):
+                        value = buffer[i, pl.ds(216 * d + 24 * q, 24), :]
+                        return value[0:16], value[16:24]
+
+                    value = yield from apply_jacobian(b + i, load)
                     if degree < NORDER - 2:
-                        series[degree, b + i] = value
+                        sources_of[degree + 1][b + i] = value
                     else:
-                        finish(b + i, [field[b + i], series[0, b + i], series[1, b + i], value])
-
-            def prepare(b, many, degree=degree):
-                turn(source(degree), b, many)
-
-            last = pipelined(prepare, use, start, blocks)
-            if degree < NORDER - 2 and blocks > 2:
-                last()
-                turn(source(degree + 1), start, 2)
-            else:
-                last()
+                        finish(b + i, [field[b + i], series0[b + i], series1[b + i], value])
+
+            def prepare(b, buffer, degree=degree):
+                return turn(sources_of[degree], b, buffer)
+
+            def then(buffer, degree=degree):
                 if degree < NORDER - 2:
-                    turn(source(degree + 1), start, 2)
+                    yield from turn(sources_of[degree + 1], start, buffer)
+
+            buffers = alternate(prepare, use, start, blocks, buffers, then, 3)
 
     def weighted(factors, members):
         total = factors[0] * members[0]
@@ -385,10 +413,7 @@
         first[b] = weighted(to_first, members)
         second[b] = weighted(to_slow, members)
 
-    build_constants(
-        deriv_ref, stiff_ref, eval_ref, lift_ref, pred4, pred1, stiff4, stiff1, lift4, lift1, table
-    )
-    lax.fori_loop(0, 8, pair_block, 0)
+    predict(present, 0, KEPT_BLOCKS, finish_first)
 
     for copy in moves:
         copy.wait()
@@ -437,15 +462,16 @@
         asked = asked + dot_nt(text.astype(BF16), chosen)
         return running + prefix[:, LANES:], asked
 
-    _, asked = lax.fori_loop(
-        0, BLOCKS, scan, (jnp.zeros((16, LANES), F32), jnp.zeros((16, ASKS), F32))
-    )
+    counted = (jnp.zeros((16, LANES), F32), jnp.zeros((16, ASKS), F32))
+    for b in range(BLOCKS):
+        counted = scan(b, counted)
+    asked = counted[1]
     asked = jnp.where(asked[2:3] > 0.5, 8.0 * asked[0:1] + asked[1:2], -1.0)
     ask_out[...] = jnp.broadcast_to(asked, (8, ASKS))
     requests = []
     for i, step in enumerate(reach):
         copy = pltpu.make_async_remote_copy(
-            src_ref=ask_out,
+            src_ref=ask_out.at[:, pl.ds(LANES * (i // 4), LANES)],
             dst_ref=ask_in.at[i],
             send_sem=ask_send.at[i],
             recv_sem=ask_recv.at[i],
@@ -455,14 +481,15 @@
         copy.start()
         requests.append(copy)
 
-    predict(present, 0, BLOCKS, finish_first)
+    predict(present, KEPT_BLOCKS, 2, finish_first)
 
     for copy in requests:
         copy.wait()
     asker = lax.broadcasted_iota(jnp.int32, (1, ASKS), 1) // REQ
     asked = jnp.full((1, ASKS), -1.0, F32)
     for i in range(len(reach)):
-        asked = jnp.where(asker == i, ask_in[i, 0:1, :], asked)
+        answer = jnp.concatenate([ask_in[i, 0:1, :]] * (ASKS // LANES), axis=1)
+        asked = jnp.where(asker == i, answer, asked)
     slots = lax.broadcasted_iota(jnp.int32, (KEEP, ASKS), 0).astype(F32)
     wanted[...] = one_hot(slots == asked)
 
@@ -494,21 +521,21 @@
             copies.append(copy)
         return copies
 
-    def table_block(b, carry):
+    def table_block(b):
         codes = info[b, pl.ds(18, 4), :]
         kinds = lax.broadcasted_iota(jnp.int32, (16, LANES), 0).astype(F32)
         chosen = jnp.concatenate([one_hot(kinds == codes[f : f + 1]) for f in range(4)], axis=1)
         value = dot(table[...], jnp.concatenate([chosen, chosen], axis=0))
         for f in range(4):
             tables[4 * b + f] = value[:, LANES * f : LANES * (f + 1)]
-        return carry
-
-    def mark_block(b, carry):
+            yield
+
+    def mark_block(b):
         _, local, _ = owners(b)
         slots = lax.broadcasted_iota(jnp.int32, (KEEP, LANES), 0).astype(F32)
         for f in range(4):
             marks[b, :, pl.ds(LANES * f, LANES)] = one_hot(slots == local[f : f + 1])
-        return carry
+            yield
 
     def receive(turn_index, copies):
         for copy in copies:
@@ -522,109 +549,132 @@
                 arrived[pl.ds(LANES * j, block.shape[0]), pl.ds(LANES * i, LANES)] = high
                 arrived[pl.ds(192 + LANES * j, block.shape[0]), pl.ds(LANES * i, LANES)] = low
 
-    def gather(b):
+    def gather(b, target):
         _, _, away = owners(b)
-        value = dot(sources[...], marks[b])
-        value = value[0:ROWS] + value[192 : 192 + ROWS]
         other = dot(arrived[...], placed[b])
         other = other[0:ROWS] + other[192 : 192 + ROWS]
+        yield
+        for half in range(2):
+            value = None
+            for start in range(0, KEEP, 256):
+                depth = pl.ds(start, min(256, KEEP - start))
+                part = dot(sources[:, depth], marks[b, depth, pl.ds(256 * half, 256)])
+                value = part if value is None else value + part
+                yield
+            value = value[0:ROWS] + value[192 : 192 + ROWS]
+            for i in range(2):
+                f = 2 * half + i
+                target[f] = jnp.where(away[f : f + 1], other, value[:, LANES * i : LANES * (i + 1)])
+                yield
+
+    def evaluate(b, outer):
         for f in range(4):
-            gathered[4 * b + f] = jnp.where(
-                away[f : f + 1], other, value[:, LANES * f : LANES * (f + 1)]
-            )
-
-    def evaluate(i):
-        total = [points[i, pl.ds(NQ * q, NQ), :] for q in range(QN)]
-        for c in range(BN):
-            column = tables[i, pl.ds(NQ * c, NQ), :]
+            i = 4 * b + f
+            total = [points[i, pl.ds(NQ * q, NQ), :] for q in range(QN)]
+            for c in range(BN):
+                column = tables[i, pl.ds(NQ * c, NQ), :]
+                for q in range(QN):
+                    row = 16 * q + c if c < 16 else TAIL + 4 * q + c - 16
+                    total[q] = total[q] + outer[f, pl.ds(row, 1), :] * column
+                yield
             for q in range(QN):
-                row = 16 * q + c if c < 16 else TAIL + 4 * q + c - 16
-                total[q] = total[q] + gathered[i, pl.ds(row, 1), :] * column
-        for q in range(QN):
-            points[i, pl.ds(NQ * q, NQ), :] = total[q]
-
-    def inside(field, b, many):
+                points[i, pl.ds(NQ * q, NQ), :] = total[q]
+
+    def inside(field, b):
         for group in range(3):
-            right = quad_rows(field, b, many, group)
+            right = quad_rows(field, b, group)
+            yield
             tall = 96 if group < 2 else 24
             wide = 64 if group < 2 else 16
             result = dot(stiff4[...] if group < 2 else stiff1[...], right)
+            yield
             for d in range(4):
-                put(turned, b, many, 216 * d + 96 * group, result[tall * d : tall * (d + 1)])
+                put(volume, b, 216 * d + 96 * group, result[tall * d : tall * (d + 1)])
+            yield
             for f in range(4):
                 part = result[4 * tall + wide * f : 4 * tall + wide * (f + 1)]
-                for i in range(many):
+                for i in range(2):
                     points[4 * (b + i) + f, pl.ds(64 * group, wide), :] = part[
                         :, LANES * i : LANES * (i + 1)
                     ]
-
-    def lift(b, many):
+            yield
+
+    def lift(b, target):
         for group in range(3):
             wide = 64 if group < 2 else 16
             for f in range(4):
-                parts = [points[4 * (b + i) + f, pl.ds(64 * group, wide), :] for i in range(many)]
-                right = parts[0] if many == 1 else jnp.concatenate(parts, axis=1)
+                parts = [points[4 * (b + i) + f, pl.ds(64 * group, wide), :] for i in range(2)]
+                right = triple(jnp.concatenate(parts, axis=1))
+                yield
                 left = lift4[f] if group < 2 else lift1[f]
-                put(faces, b, many, 216 * f + 96 * group, dot(left, triple(right)))
-
-    def change_of(b):
+                put(target, 0, 216 * f + 96 * group, dot(left, right))
+                yield
+
+    def change_of(b, face):
         def load(d, q):
-            value = turned[b, pl.ds(216 * d + 24 * q, 24), :]
+            value = volume[b, pl.ds(216 * d + 24 * q, 24), :]
             for f in range(4):
-                value = value - info[b, pl.ds(4 * d + f, 1), :] * faces[b, pl.ds(216 * f + 24 * q, 24), :]
+                value = value - info[b, pl.ds(4 * d + f, 1), :] * face[pl.ds(216 * f + 24 * q, 24), :]
             return value[0:16], value[16:24]
 
-        change = apply_jacobian(b, load)
+        change = yield from apply_jacobian(b, load)
         skew = []
         for q in range(QN):
-            value = turned[b, pl.ds(648 + 24 * q, 24), :]
+            value = volume[b, pl.ds(648 + 24 * q, 24), :]
             for f in range(4):
-                value = value - faces[b, pl.ds(216 * f + 24 * q, 24), :]
+                value = value - face[pl.ds(216 * f + 24 * q, 24), :]
             skew.append(value)
+            yield
         tails = [
             jnp.where(low_half, skew[2 * i][16:24], skew[min(2 * i + 1, 8)][16:24]) for i in range(5)
         ]
         skew = jnp.concatenate([s[0:16] for s in skew] + tails, axis=0)
         return change - info[b, pl.ds(12, 1), :] * skew
 
-    def prepare_inside(field):
+    def update(turn_index, copies, finish, later):
+        receive(turn_index, copies)
+        run(gather(0, gathered0))
+
         def step(i, carry):
-            inside(field, 2 * i, 2)
+            together(evaluate(2 * i, gathered0), gather(2 * i + 1, gathered1), 6)
+            together(evaluate(2 * i + 1, gathered1), gather(2 * i + 2, gathered0), 6)
             return carry
 
         lax.fori_loop(0, BLOCKS // 2, step, 0)
-        inside(field, BLOCKS - 1, 1)
-
-    def update(turn_index, copies, finish):
-        receive(turn_index, copies)
-        gather(0)
-
-        def step(b, carry):
-            for f in range(4):
-                evaluate(4 * b + f)
-            gather(b + 1)
-            return carry
-
-        lax.fori_loop(0, BLOCKS - 1, step, 0)
-        for f in range(4):
-            evaluate(4 * (BLOCKS - 1) + f)
-        lift(0, 2)
-
-        def use(b, many):
+        together(evaluate(BLOCKS - 1, gathered0), lift(0, faces0), 4)
+
+        def use(b, many, face):
             for i in range(many):
-                finish(b + i, change_of(b + i))
-
-        pipelined(lift, use, 0, BLOCKS)()
+                change = yield from change_of(b + i, face.at[i])
+                finish(b + i, change)
+
+        if not later:
+            alternate(lift, use, 0, BLOCKS, (faces0, faces1), lambda buffer: iter(()), 3)
+            return None
+        rest = alternate(lift, use, 0, KEPT_BLOCKS, (faces0, faces1), lambda buffer: lift(KEPT_BLOCKS, buffer), 3)
+        return use(KEPT_BLOCKS, 2, rest[0])
 
     copies = exchange(first, 0)
-    lax.fori_loop(0, BLOCKS, table_block, 0)
-    lax.fori_loop(0, BLOCKS, mark_block, 0)
-    prepare_inside(first)
+
+    def tables_and_inside(i):
+        yield from table_block(2 * i)
+        yield from table_block(2 * i + 1)
+        yield from inside(first, 2 * i)
+
+    def mark_pair(i):
+        yield from mark_block(2 * i)
+        yield from mark_block(2 * i + 1)
+
+    def ready(i, carry):
+        together(tables_and_inside(i), mark_pair(i), 2)
+        return carry
+
+    lax.fori_loop(0, BLOCKS // 2 + 1, ready, 0)
 
     def finish_middle(b, change):
         base[b] = present[b] + change
 
-    update(0, copies, finish_middle)
+    rest = update(0, copies, finish_middle, True)
 
     def finish_second(b, members):
         quick = info[b, pl.ds(13, 1), :] < 0.5
@@ -632,8 +682,14 @@
 
     predict(base, 0, KEPT_BLOCKS, finish_second)
     copies = exchange(second, 1)
+    run(rest)
     predict(base, KEPT_BLOCKS, 2, finish_second)
-    prepare_inside(second)
+
+    def inside_pair(i, carry):
+        run(inside(second, 2 * i))
+        return carry
+
+    lax.fori_loop(0, BLOCKS // 2 + 1, inside_pair, 0)
 
     def finish_last(b, change):
         value = jnp.where(info[b, pl.ds(22, 1), :] > 0.5, base[b] + change, 0.0)
@@ -642,7 +698,7 @@
             out_ref[q, 0:16, at] = value[16 * q : 16 * q + 16]
             out_ref[q, 16:20, at] = value[TAIL + 4 * q : TAIL + 4 * q + 4]
 
-    update(1, copies, finish_last)
+    update(1, copies, finish_last, False)
 
 
 def per_device(
@@ -676,26 +732,31 @@
             pltpu.VMEM((BN * NQ, 32), BF16),
             pltpu.VMEM((QN, QN, 3, PARTITION_SLOTS), F32),
             pltpu.VMEM((BLOCKS, 27, 5, 8, LANES), F32),
-            pltpu.VMEM((BLOCKS, 24, LANES), F32),
-            pltpu.VMEM((BLOCKS, ROWS, LANES), F32),
-            pltpu.VMEM((BLOCKS, ROWS, LANES), F32),
-            pltpu.VMEM((BLOCKS, ROWS, LANES), F32),
-            pltpu.VMEM((BLOCKS, ROWS, LANES), F32),
-            pltpu.VMEM((2, BLOCKS, ROWS, LANES), F32),
-            pltpu.VMEM((BLOCKS, 864, LANES), F32),
-            pltpu.VMEM((BLOCKS, 864, LANES), F32),
-            pltpu.VMEM((4 * BLOCKS, TAIL, LANES), F32),
-            pltpu.VMEM((4 * BLOCKS, ROWS, LANES), F32),
-            pltpu.VMEM((4 * BLOCKS, BN * NQ, LANES), F32),
+            pltpu.VMEM((BLOCKS + 1, 24, LANES), F32),
+            pltpu.VMEM((BLOCKS + 1, ROWS, LANES), F32),
+            pltpu.VMEM((BLOCKS + 1, ROWS, LANES), F32),
+            pltpu.VMEM((BLOCKS + 1, ROWS, LANES), F32),
+            pltpu.VMEM((BLOCKS + 1, ROWS, LANES), F32),
+            pltpu.VMEM((BLOCKS + 1, ROWS, LANES), F32),
+            pltpu.VMEM((BLOCKS + 1, ROWS, LANES), F32),
+            pltpu.VMEM((2, 648, LANES), F32),
+            pltpu.VMEM((2, 648, LANES), F32),
+            pltpu.VMEM((BLOCKS + 1, 864, LANES), F32),
+            pltpu.VMEM((2, 864, LANES), F32),
+            pltpu.VMEM((2, 864, LANES), F32),
+            pltpu.VMEM((4 * BLOCKS + 4, TAIL, LANES), F32),
+            pltpu.VMEM((4, ROWS, LANES), F32),
+            pltpu.VMEM((4, ROWS, LANES), F32),
+            pltpu.VMEM((4 * BLOCKS + 4, BN * NQ, LANES), F32),
             pltpu.VMEM((384, KEEP), BF16),
-            pltpu.VMEM((BLOCKS, KEEP, 4 * LANES), BF16),
+            pltpu.VMEM((BLOCKS + 1, KEEP, 4 * LANES), BF16),
             pltpu.VMEM((KEEP, ASKS), BF16),
             pltpu.VMEM((BLOCKS, ASKS, LANES), BF16),
             pltpu.VMEM((384, ASKS), BF16),
             pltpu.VMEM((SLAB, LANES), F32),
             pltpu.VMEM((2, LANES, SLAB), F32),
             pltpu.VMEM((8, ASKS), F32),
-            pltpu.VMEM((9, 8, ASKS), F32),
+            pltpu.VMEM((9, 8, LANES), F32),
             pltpu.VMEM((2, ASKS, 256), F32),
             pltpu.VMEM((2, ASKS, 256), F32),
             pltpu.SemaphoreType.DMA,
@@ -707,7 +768,7 @@
             pltpu.SemaphoreType.DMA((2, 9)),
         ],
         compiler_params=pltpu.CompilerParams(
-            collective_id=0, has_side_effects=True, vmem_limit_bytes=60 << 20
+            collective_id=0, has_side_effects=True, vmem_limit_bytes=56 << 20
         ),
     )(
         element_freedom_values,

time: 79.4 us -> 76.8 us (0.967)
  Pallas kernels: 77 us -> 74.4 us
    pallas_call x1, Pallas kernels: 77 us -> 74.4 us  [per_device(): pl.pallas_call(functools.partial(kernel, count), out_shape=jax.ShapeDtype...]
where the time goes in v3:
time: 76.8 us; the launch traced here: 76.6 us
  Pallas kernels  74.4 us (97%)
  local copies, waits for them, and re-layouts  2.22 us (3%)
    pallas_call x1, Pallas kernels, per_device(): pl.pallas_call(functools.partial(kernel, count), out_shape=jax.ShapeDtype...  74.4 us
    unnamed x1, local copies, waits for them, and re-layouts  2.22 us

profile of v3, /device:TPU:1, one launch (start us, length us, event | category | flops | bytes accessed | tf_op | source)
XLA Modules:
  0.0 76.6 jit_solution(6840667899186989573)
XLA Ops:
  0.0 74.4 %shard_map.118 = f32[9,20,1152]{2,1,0:T(8,128)} custom-call(f32[9,20,1024]{2,1,0:T(8,128)} %x_ref.1, f32[9,9,3,1024]{3,2,1,0:T(4,128)} %bitcast.6, f32[3,4,1024]{2,1,0:T(4,128)} %bitcast.8, f32[1,1024]{1,0:T(1,128)} %bitcast.9, s32[1,1024]{1,0:T(1,128)} %bitcast.10, s32[1,1024]{1,0:T(1,128)} %bitcast.11, s32[4,1024]{1,0:T(4,128)} %link_ref.1, ...), custom_call_target="tpu_custom_call" | custom-call | tf_op jit(solution)/shard_map/pallas_call | solution.py:720
  74.4 2.2 %copy.14 = f32[9,20,1152]{2,1,0:T(8,128)} copy(f32[9,20,1152]{2,1,0:T(8,128)} %shard_map.118) | data formatting | bytes 1658880

commit v4 on v3

--- a/solution.py
+++ b/solution.py
@@ -636,8 +636,8 @@
         run(gather(0, gathered0))
 
         def step(i, carry):
-            together(evaluate(2 * i, gathered0), gather(2 * i + 1, gathered1), 6)
-            together(evaluate(2 * i + 1, gathered1), gather(2 * i + 2, gathered0), 6)
+            together(evaluate(2 * i, gathered0), gather(2 * i + 1, gathered1), 8)
+            together(evaluate(2 * i + 1, gathered1), gather(2 * i + 2, gathered0), 8)
             return carry
 
         lax.fori_loop(0, BLOCKS // 2, step, 0)

time: 76.8 us -> 76.8 us (level)
  no operation moved by 1% of the time
where the time goes in v4:
time: 76.8 us; the launch traced here: 76.6 us
  Pallas kernels  74.4 us (97%)
  local copies, waits for them, and re-layouts  2.22 us (3%)
    pallas_call x1, Pallas kernels, per_device(): pl.pallas_call(functools.partial(kernel, count), out_shape=jax.ShapeDtype...  74.4 us
    unnamed x1, local copies, waits for them, and re-layouts  2.22 us

profile of v4, /device:TPU:1, one launch (start us, length us, event | category | flops | bytes accessed | tf_op | source)
XLA Modules:
  0.0 76.6 jit_solution(6840667899186989573)
XLA Ops:
  0.0 74.4 %shard_map.118 = f32[9,20,1152]{2,1,0:T(8,128)} custom-call(f32[9,20,1024]{2,1,0:T(8,128)} %x_ref.1, f32[9,9,3,1024]{3,2,1,0:T(4,128)} %bitcast.6, f32[3,4,1024]{2,1,0:T(4,128)} %bitcast.8, f32[1,1024]{1,0:T(1,128)} %bitcast.9, s32[1,1024]{1,0:T(1,128)} %bitcast.10, s32[1,1024]{1,0:T(1,128)} %bitcast.11, s32[4,1024]{1,0:T(4,128)} %link_ref.1, ...), custom_call_target="tpu_custom_call" | custom-call | tf_op jit(solution)/shard_map/pallas_call | solution.py:720
  74.4 2.2 %copy.14 = f32[9,20,1152]{2,1,0:T(8,128)} copy(f32[9,20,1152]{2,1,0:T(8,128)} %shard_map.118) | data formatting | bytes 1658880
